TPU v7x, 32 devices: a whole 2x2x4 slice. The times are simulated.
32 devices in a mesh: req: 8 (over z, y), tp: 4 (over x, core).
Axes of the slice: x: 2, y: 2, z: 4, core: 2. Of those that a mesh axis runs over, the one named last changes fastest.
Arguments:
- tokens: bfloat16 [4096, 2048], P('req')
- token_request_number: int32 [8, 512], P('req'), may hold values from 0 to 7, never falling along the last dimension, each value on 1 to 256 neighbouring positions
- request_adapter_position: int32 [8, 8], P('req'), may hold values from 0 to 15
- adapters_in_use: int32 [16], replicated, may hold values from 0 to 15, as said below
- adapter_storage_slot: int32 [16], replicated, may hold values from 0 to 15, each once
- input_norm_gain: bfloat16 [2048], replicated, may hold values from 0.5 to 1.5
- query_weight: bfloat16 [2048, 2048], P('req', 'tp')
- key_weight: bfloat16 [2048, 2048], P('req', 'tp')
- value_weight: bfloat16 [2048, 2048], P('req', 'tp'), may hold values from -0.125 to 0.125
- output_weight: bfloat16 [2048, 2048], P('tp', 'req'), may hold values from -0.125 to 0.125
- adapter_down_weight: bfloat16 [16, 2, 16, 2048], P('req'), may hold values from -0.125 to 0.125
- adapter_up_weight: bfloat16 [16, 2, 16, 2048], P('req', None, None, 'tp'), may hold values from -0.75 to 0.75
Outputs:
- layer_out: bfloat16 [4096, 2048], P('req', 'tp')
Inputs may be any that keep to these rules, and one draw needn't show every extreme that they name: `adapters_in_use`: 16 different adapter numbers; 0 and 15 are always among them. `token_request_number`: the 512 tokens of each index of req form exactly 8 requests in order, each of 1 to 256 tokens, and one of exactly 256.
All inputs are finite; a program needn't handle non-finite values.
Results may differ from a plain program's by a relative error of at most 0.01.
Values may be sent and summed in bfloat16 or wider, within the bound.
A program may use at most 64 MiB of HBM per device.

v0:
```python
import jax
import jax.numpy as jnp
from jax import lax
from jax.sharding import PartitionSpec as P

HEAD_WIDTH = 64


norm_eps = 1e-05
rope_base = 130000.0
adapter_scale = 2.0


def spread_2(value, axis, root):
    mine = lax.axis_index(axis) == root
    return lax.psum(jnp.where(mine, value, jnp.zeros_like(value)), axis)


def positions_of(segment):
    ordinal = jnp.arange(segment.shape[0], dtype=jnp.int32)
    starts = jnp.concatenate([jnp.ones((1,), jnp.bool_), segment[1:] != segment[:-1]])
    segment_start = lax.cummax(jnp.where(starts, ordinal, jnp.zeros_like(ordinal)), axis=0)
    return ordinal - segment_start


def apply_rotation(values, token_positions):
    half_dim = HEAD_WIDTH // 2
    frequency = rope_base ** (-(jnp.arange(half_dim, dtype=jnp.float32) * 2.0 / HEAD_WIDTH))
    angles = token_positions.astype(jnp.float32)[:, None] * frequency[None, :]
    cosine = jnp.cos(angles)[:, None, :]
    sine_part = jnp.sin(angles)[:, None, :]
    first_half = values[..., :half_dim]
    second_half = values[..., half_dim:]
    return jnp.concatenate(
        [
            first_half * cosine - second_half * sine_part,
            second_half * cosine + first_half * sine_part,
        ],
        axis=-1,
    )


def attend(query_per_head, key_heads, value_per_head, segment):
    scores = (
        jnp.einsum("qhd,khd->hqk", query_per_head, key_heads, preferred_element_type=jnp.float32)
        * 0.125
    )
    ordinal = jnp.arange(segment.shape[0], dtype=jnp.int32)
    allowed = (segment[:, None] == segment[None, :]) & (ordinal[None, :] <= ordinal[:, None])
    scores = jnp.where(allowed[None], scores, jnp.float32(-1e30))
    row_peak = jnp.max(scores, axis=-1, keepdims=True)
    exponent = jnp.where(allowed[None], jnp.exp(scores - row_peak), jnp.float32(0.0))
    weights = (exponent / jnp.sum(exponent, axis=-1, keepdims=True)).astype(jnp.bfloat16)
    return jnp.einsum(
        "hqk,khd->qhd", weights, value_per_head, preferred_element_type=jnp.float32
    ).astype(jnp.bfloat16)


def local(
    tokens,
    token_request_number,
    request_adapter_position,
    adapters_in_use,
    adapter_storage_slot,
    input_norm_gain,
    query_weight,
    key_weight,
    value_weight,
    output_weight,
    adapter_down_weight,
    adapter_up_weight,
):
    row_total, model_width = tokens.shape
    local_width = query_weight.shape[1]
    reduced_rows = adapter_down_weight.shape[2]
    active_count = adapters_in_use.shape[0]
    slot_total = adapter_down_weight.shape[0]
    segment = token_request_number[0]
    request_adapters = request_adapter_position[0]
    storage_slots = jnp.take(adapter_storage_slot, adapters_in_use, axis=0)
    stored_weight = jnp.concatenate([adapter_down_weight, adapter_up_weight], axis=3)

    def fetch_one(active_index, fetched):
        home = storage_slots[active_index]
        own_slot = lax.dynamic_index_in_dim(stored_weight, home % slot_total, 0, keepdims=False)
        received = spread_2(own_slot, "req", home // slot_total)
        return lax.dynamic_update_index_in_dim(fetched, received, active_index, 0)

    fetched = lax.fori_loop(
        0,
        active_count,
        fetch_one,
        jnp.zeros((active_count,) + stored_weight.shape[1:], jnp.bfloat16),
    )
    fetch_down = fetched[..., :model_width]
    fetch_up = fetched[..., model_width:]
    floats = tokens.astype(jnp.float32)
    normed = (
        floats
        * lax.rsqrt(jnp.mean(floats * floats, axis=-1, keepdims=True) + norm_eps)
        * input_norm_gain.astype(jnp.float32)
    ).astype(jnp.bfloat16)
    query_plain = jnp.dot(
        normed,
        lax.all_gather(query_weight, "req", axis=0, tiled=True),
        preferred_element_type=jnp.float32,
    )
    key_base = jnp.dot(
        normed,
        lax.all_gather(key_weight, "req", axis=0, tiled=True),
        preferred_element_type=jnp.float32,
    )
    value_plain = jnp.dot(
        normed,
        lax.all_gather(value_weight, "req", axis=0, tiled=True),
        preferred_element_type=jnp.float32,
    )
    request_total = request_adapters.shape[0]
    member = segment[:, None] == jnp.arange(request_total, dtype=jnp.int32)[None, :]
    token_adapter = jnp.sum(
        jnp.where(member, request_adapters[None, :], jnp.zeros_like(request_adapters)[None, :]),
        axis=1,
    )
    select = token_adapter[:, None] == jnp.arange(active_count, dtype=jnp.int32)[None, :]
    shrunk_all = lax.dot_general(
        normed,
        fetch_down.reshape(active_count * 2 * reduced_rows, model_width),
        (((1,), (1,)), ((), ())),
        preferred_element_type=jnp.float32,
    )
    shrunk_all = shrunk_all.reshape(row_total, active_count, 2, reduced_rows)
    shrunk = jnp.sum(
        jnp.where(select[:, :, None, None], shrunk_all, jnp.float32(0.0)), axis=1
    ).astype(jnp.bfloat16)
    spread = jnp.where(select[:, :, None, None], shrunk[:, None, :, :], jnp.zeros((), jnp.bfloat16))
    query_change = jnp.dot(
        spread[:, :, 0, :].reshape(row_total, active_count * reduced_rows),
        fetch_up[:, 0].reshape(active_count * reduced_rows, local_width),
        preferred_element_type=jnp.float32,
    )
    value_change = jnp.dot(
        spread[:, :, 1, :].reshape(row_total, active_count * reduced_rows),
        fetch_up[:, 1].reshape(active_count * reduced_rows, local_width),
        preferred_element_type=jnp.float32,
    )
    head_total = local_width // HEAD_WIDTH
    token_positions = positions_of(segment)
    query_per_head = apply_rotation(
        (query_plain + adapter_scale * query_change).reshape(row_total, head_total, HEAD_WIDTH),
        token_positions,
    ).astype(jnp.bfloat16)
    key_heads = apply_rotation(
        key_base.reshape(row_total, head_total, HEAD_WIDTH), token_positions
    ).astype(jnp.bfloat16)
    value_per_head = (
        (value_plain + adapter_scale * value_change)
        .astype(jnp.bfloat16)
        .reshape(row_total, head_total, HEAD_WIDTH)
    )
    attended = attend(query_per_head, key_heads, value_per_head, segment).reshape(
        row_total, local_width
    )
    partial_out = jnp.dot(
        attended,
        lax.all_gather(output_weight, "req", axis=1, tiled=True),
        preferred_element_type=jnp.float32,
    )
    summed = lax.psum_scatter(
        partial_out.astype(jnp.bfloat16), "tp", scatter_dimension=1, tiled=True
    ).astype(jnp.float32)
    share_width = summed.shape[1]
    residual_part = lax.dynamic_slice_in_dim(
        tokens, lax.axis_index("tp") * share_width, share_width, 1
    )
    return (summed + residual_part.astype(jnp.float32)).astype(jnp.bfloat16)


def solution(mesh):
    in_specs = (
        P("req", None),
        P("req", None),
        P("req", None),
        P(),
        P(),
        P(),
        P("req", "tp"),
        P("req", "tp"),
        P("req", "tp"),
        P("tp", "req"),
        P("req", None, None, None),
        P("req", None, None, "tp"),
    )
    out_specs = P("req", "tp")
    return jax.shard_map(local, mesh=mesh, in_specs=in_specs, out_specs=out_specs, check_vma=False)
```

profile of v0, /device:TPU:0, one launch (start us, length us, event | category | flops | bytes accessed | tf_op | source)
XLA Modules:
  0.0 1461.1 jit_solution(2238570392540167822)
XLA Ops:
  10.6 1205.2 %while.15 = (s32[]{:T(128)}, bf16[16,2,16,2560]{3,2,1,0:T(8,128)(2,1)}, s32[16]{0:T(128)S(1)}, bf16[2,2,16,2560]{3,2,1,0:T(8,128)(2,1)S(1)}, s32[]{:T(128)}, /*i...) while((s32[]{:T(128)}, bf16[16,2,16,2560]{3,2,1,0:T(8,128)(2,1)}, s32[16]{0:T(128)S(1)}, ...), condition=%wide.region_4.5_spmd, body=%wide.region_2.4_spmd.sunk | while | flops 163868 | bytes 1638832 | solution.py:89
  14.5 72.8 %all-reduce.2.cloned.1.call-done = bf16[1,2,16,2560]{3,2,1,0:T(8,128)(2,1)} async-done(((bf16[1,2,16,2560]{3,2,1,0:T(8,128)(2,1)}), bf16[1,2,16,2560]{3,2,1,0:T(8,128)(2,1)}) %all-reduce.2.cloned.1.call-update) | async-done | bytes 163856 | tf_op jit(solution)/shard_map/while/body/eval_jaxpr/psum | solution.py:16
  87.3 1.6 constant_dynamic-update-slice_fusion.2
  92.8 69.8 %all-reduce.2.cloned.1.call-done = bf16[1,2,16,2560]{3,2,1,0:T(8,128)(2,1)} async-done(((bf16[1,2,16,2560]{3,2,1,0:T(8,128)(2,1)}), bf16[1,2,16,2560]{3,2,1,0:T(8,128)(2,1)}) %all-reduce.2.cloned.1.call-update) | async-done | bytes 163856 | tf_op jit(solution)/shard_map/while/body/eval_jaxpr/psum | solution.py:16
  162.6 1.6 constant_dynamic-update-slice_fusion.2
  168.1 69.8 %all-reduce.2.cloned.1.call-done = bf16[1,2,16,2560]{3,2,1,0:T(8,128)(2,1)} async-done(((bf16[1,2,16,2560]{3,2,1,0:T(8,128)(2,1)}), bf16[1,2,16,2560]{3,2,1,0:T(8,128)(2,1)}) %all-reduce.2.cloned.1.call-update) | async-done | bytes 163856 | tf_op jit(solution)/shard_map/while/body/eval_jaxpr/psum | solution.py:16
  237.8 1.6 constant_dynamic-update-slice_fusion.2
  243.3 69.5 %all-reduce.2.cloned.1.call-done = bf16[1,2,16,2560]{3,2,1,0:T(8,128)(2,1)} async-done(((bf16[1,2,16,2560]{3,2,1,0:T(8,128)(2,1)}), bf16[1,2,16,2560]{3,2,1,0:T(8,128)(2,1)}) %all-reduce.2.cloned.1.call-update) | async-done | bytes 163856 | tf_op jit(solution)/shard_map/while/body/eval_jaxpr/psum | solution.py:16
  312.8 1.6 constant_dynamic-update-slice_fusion.2
  318.3 69.5 %all-reduce.2.cloned.1.call-done = bf16[1,2,16,2560]{3,2,1,0:T(8,128)(2,1)} async-done(((bf16[1,2,16,2560]{3,2,1,0:T(8,128)(2,1)}), bf16[1,2,16,2560]{3,2,1,0:T(8,128)(2,1)}) %all-reduce.2.cloned.1.call-update) | async-done | bytes 163856 | tf_op jit(solution)/shard_map/while/body/eval_jaxpr/psum | solution.py:16
  387.8 1.6 constant_dynamic-update-slice_fusion.2
  393.3 69.5 %all-reduce.2.cloned.1.call-done = bf16[1,2,16,2560]{3,2,1,0:T(8,128)(2,1)} async-done(((bf16[1,2,16,2560]{3,2,1,0:T(8,128)(2,1)}), bf16[1,2,16,2560]{3,2,1,0:T(8,128)(2,1)}) %all-reduce.2.cloned.1.call-update) | async-done | bytes 163856 | tf_op jit(solution)/shard_map/while/body/eval_jaxpr/psum | solution.py:16
  462.8 1.6 constant_dynamic-update-slice_fusion.2
  468.3 69.8 %all-reduce.2.cloned.1.call-done = bf16[1,2,16,2560]{3,2,1,0:T(8,128)(2,1)} async-done(((bf16[1,2,16,2560]{3,2,1,0:T(8,128)(2,1)}), bf16[1,2,16,2560]{3,2,1,0:T(8,128)(2,1)}) %all-reduce.2.cloned.1.call-update) | async-done | bytes 163856 | tf_op jit(solution)/shard_map/while/body/eval_jaxpr/psum | solution.py:16
  538.1 1.6 constant_dynamic-update-slice_fusion.2
  543.6 69.8 %all-reduce.2.cloned.1.call-done = bf16[1,2,16,2560]{3,2,1,0:T(8,128)(2,1)} async-done(((bf16[1,2,16,2560]{3,2,1,0:T(8,128)(2,1)}), bf16[1,2,16,2560]{3,2,1,0:T(8,128)(2,1)}) %all-reduce.2.cloned.1.call-update) | async-done | bytes 163856 | tf_op jit(solution)/shard_map/while/body/eval_jaxpr/psum | solution.py:16
  613.4 1.6 constant_dynamic-update-slice_fusion.2
  618.9 69.8 %all-reduce.2.cloned.1.call-done = bf16[1,2,16,2560]{3,2,1,0:T(8,128)(2,1)} async-done(((bf16[1,2,16,2560]{3,2,1,0:T(8,128)(2,1)}), bf16[1,2,16,2560]{3,2,1,0:T(8,128)(2,1)}) %all-reduce.2.cloned.1.call-update) | async-done | bytes 163856 | tf_op jit(solution)/shard_map/while/body/eval_jaxpr/psum | solution.py:16
  688.7 1.6 constant_dynamic-update-slice_fusion.2
  694.2 69.5 %all-reduce.2.cloned.1.call-done = bf16[1,2,16,2560]{3,2,1,0:T(8,128)(2,1)} async-done(((bf16[1,2,16,2560]{3,2,1,0:T(8,128)(2,1)}), bf16[1,2,16,2560]{3,2,1,0:T(8,128)(2,1)}) %all-reduce.2.cloned.1.call-update) | async-done | bytes 163856 | tf_op jit(solution)/shard_map/while/body/eval_jaxpr/psum | solution.py:16
  763.6 1.6 constant_dynamic-update-slice_fusion.2
  769.1 69.8 %all-reduce.2.cloned.1.call-done = bf16[1,2,16,2560]{3,2,1,0:T(8,128)(2,1)} async-done(((bf16[1,2,16,2560]{3,2,1,0:T(8,128)(2,1)}), bf16[1,2,16,2560]{3,2,1,0:T(8,128)(2,1)}) %all-reduce.2.cloned.1.call-update) | async-done | bytes 163856 | tf_op jit(solution)/shard_map/while/body/eval_jaxpr/psum | solution.py:16
  838.9 1.6 constant_dynamic-update-slice_fusion.2
  844.4 69.5 %all-reduce.2.cloned.1.call-done = bf16[1,2,16,2560]{3,2,1,0:T(8,128)(2,1)} async-done(((bf16[1,2,16,2560]{3,2,1,0:T(8,128)(2,1)}), bf16[1,2,16,2560]{3,2,1,0:T(8,128)(2,1)}) %all-reduce.2.cloned.1.call-update) | async-done | bytes 163856 | tf_op jit(solution)/shard_map/while/body/eval_jaxpr/psum | solution.py:16
  913.9 1.6 constant_dynamic-update-slice_fusion.2
  919.4 69.8 %all-reduce.2.cloned.1.call-done = bf16[1,2,16,2560]{3,2,1,0:T(8,128)(2,1)} async-done(((bf16[1,2,16,2560]{3,2,1,0:T(8,128)(2,1)}), bf16[1,2,16,2560]{3,2,1,0:T(8,128)(2,1)}) %all-reduce.2.cloned.1.call-update) | async-done | bytes 163856 | tf_op jit(solution)/shard_map/while/body/eval_jaxpr/psum | solution.py:16
  989.2 1.6 constant_dynamic-update-slice_fusion.2
  994.7 69.5 %all-reduce.2.cloned.1.call-done = bf16[1,2,16,2560]{3,2,1,0:T(8,128)(2,1)} async-done(((bf16[1,2,16,2560]{3,2,1,0:T(8,128)(2,1)}), bf16[1,2,16,2560]{3,2,1,0:T(8,128)(2,1)}) %all-reduce.2.cloned.1.call-update) | async-done | bytes 163856 | tf_op jit(solution)/shard_map/while/body/eval_jaxpr/psum | solution.py:16
  1064.2 1.6 constant_dynamic-update-slice_fusion.2
  1069.7 69.5 %all-reduce.2.cloned.1.call-done = bf16[1,2,16,2560]{3,2,1,0:T(8,128)(2,1)} async-done(((bf16[1,2,16,2560]{3,2,1,0:T(8,128)(2,1)}), bf16[1,2,16,2560]{3,2,1,0:T(8,128)(2,1)}) %all-reduce.2.cloned.1.call-update) | async-done | bytes 163856 | tf_op jit(solution)/shard_map/while/body/eval_jaxpr/psum | solution.py:16
  1139.1 1.6 constant_dynamic-update-slice_fusion.2
  1144.6 69.5 %all-reduce.2.cloned.1.call-done = bf16[1,2,16,2560]{3,2,1,0:T(8,128)(2,1)} async-done(((bf16[1,2,16,2560]{3,2,1,0:T(8,128)(2,1)}), bf16[1,2,16,2560]{3,2,1,0:T(8,128)(2,1)}) %all-reduce.2.cloned.1.call-update) | async-done | bytes 163856 | tf_op jit(solution)/shard_map/while/body/eval_jaxpr/psum | solution.py:16
  1214.1 1.6 constant_dynamic-update-slice_fusion.2
  1219.9 3.0 fusion.23
  1223.9 43.4 %all-gather.5.cloned.1.call-done = bf16[2048,512]{1,0:T(8,128)(2,1)} async-done(((bf16[256,512]{1,0:T(8,128)(2,1)}), bf16[2048,512]{1,0:T(8,128)(2,1)}) %all-gather.5.cloned.1.call-update) | async-done | bytes 2097168 | tf_op jit(solution)/shard_map/all_gather | solution.py:115
  1267.3 3.0 fusion.44
  1270.4 2.1 fusion.22
  1272.5 44.6 %all-gather.7.cloned.1.call-done = bf16[2048,512]{1,0:T(8,128)(2,1)} async-done(((bf16[256,512]{1,0:T(8,128)(2,1)}), bf16[2048,512]{1,0:T(8,128)(2,1)}) %all-gather.7.cloned.1.call-update) | async-done | bytes 2097168 | tf_op jit(solution)/shard_map/all_gather | solution.py:105
  1317.1 3.1 fusion.41
  1320.2 1.3 fusion.20
  1321.5 45.3 %all-gather.9.cloned.1.call-done = bf16[2048,512]{1,0:T(8,128)(2,1)} async-done(((bf16[256,512]{1,0:T(8,128)(2,1)}), bf16[2048,512]{1,0:T(8,128)(2,1)}) %all-gather.9.cloned.1.call-update) | async-done | bytes 2097168 | tf_op jit(solution)/shard_map/all_gather | solution.py:110
  1366.8 3.0 fusion.39
  1371.1 8.1 fusion.46
  1379.2 4.3 fusion.21
  1383.5 34.4 %all-gather.11.cloned.1.call-done = bf16[512,2048]{1,0:T(8,128)(2,1)} async-done(((bf16[512,256]{1,0:T(8,128)(2,1)}), bf16[512,2048]{1,0:T(8,128)(2,1)}) %all-gather.11.cloned.1.call-update) | async-done | bytes 2097168 | tf_op jit(solution)/shard_map/all_gather | solution.py:165
  1417.9 4.2 convolution_convert_fusion
  1422.2 29.6 %reduce-scatter.2.cloned.1.call-done = bf16[512,512]{1,0:T(8,128)(2,1)} async-done(((bf16[512,2048]{1,0:T(8,128)(2,1)}), bf16[512,512]{1,0:T(8,128)(2,1)}) %reduce-scatter.2.cloned.1.call-update) | async-done | bytes 524304 | tf_op jit(solution)/shard_map/reduce_scatter | solution.py:168
  1451.8 2.0 add_convert_fusion
  (113 shorter events, 30.2 us)
Async XLA Ops:
  7.4 0.7 copy-start
  9.4 1208.9 %copy-start.1 = (bf16[512,2048]{1,0:T(8,128)(2,1)S(1)}, bf16[512,2048]{1,0:T(8,128)(2,1)}, u32[]{:S(2)}) copy-start(bf16[512,2048]{1,0:T(8,128)(2,1)} %param.14) | copy-start | bytes 6291460
  10.5 1207.7 %copy-start.6 = (bf16[2048]{0:T(1024)(128)(2,1)S(1)}, bf16[2048]{0:T(1024)(128)(2,1)}, u32[]{:S(2)}) copy-start(bf16[2048]{0:T(1024)(128)(2,1)} %param.19) | copy-start | bytes 12292
  10.6 76.7 %all-reduce.2.cloned.1.call-start = ((), (), s32[]{:S(2)}) async-start(), calls=%async_computation.6 | async-start | bytes 327680 | tf_op jit(solution)/shard_map/while/body/eval_jaxpr/psum | solution.py:16
  88.9 73.7 %all-reduce.2.cloned.1.call-start = ((), (), s32[]{:S(2)}) async-start(), calls=%async_computation.6 | async-start | bytes 327680 | tf_op jit(solution)/shard_map/while/body/eval_jaxpr/psum | solution.py:16
  164.2 73.7 %all-reduce.2.cloned.1.call-start = ((), (), s32[]{:S(2)}) async-start(), calls=%async_computation.6 | async-start | bytes 327680 | tf_op jit(solution)/shard_map/while/body/eval_jaxpr/psum | solution.py:16
  239.4 73.4 %all-reduce.2.cloned.1.call-start = ((), (), s32[]{:S(2)}) async-start(), calls=%async_computation.6 | async-start | bytes 327680 | tf_op jit(solution)/shard_map/while/body/eval_jaxpr/psum | solution.py:16
  314.4 73.4 %all-reduce.2.cloned.1.call-start = ((), (), s32[]{:S(2)}) async-start(), calls=%async_computation.6 | async-start | bytes 327680 | tf_op jit(solution)/shard_map/while/body/eval_jaxpr/psum | solution.py:16
  389.4 73.4 %all-reduce.2.cloned.1.call-start = ((), (), s32[]{:S(2)}) async-start(), calls=%async_computation.6 | async-start | bytes 327680 | tf_op jit(solution)/shard_map/while/body/eval_jaxpr/psum | solution.py:16
  464.4 73.7 %all-reduce.2.cloned.1.call-start = ((), (), s32[]{:S(2)}) async-start(), calls=%async_computation.6 | async-start | bytes 327680 | tf_op jit(solution)/shard_map/while/body/eval_jaxpr/psum | solution.py:16
  539.7 73.7 %all-reduce.2.cloned.1.call-start = ((), (), s32[]{:S(2)}) async-start(), calls=%async_computation.6 | async-start | bytes 327680 | tf_op jit(solution)/shard_map/while/body/eval_jaxpr/psum | solution.py:16
  615.0 73.7 %all-reduce.2.cloned.1.call-start = ((), (), s32[]{:S(2)}) async-start(), calls=%async_computation.6 | async-start | bytes 327680 | tf_op jit(solution)/shard_map/while/body/eval_jaxpr/psum | solution.py:16
  690.2 73.4 %all-reduce.2.cloned.1.call-start = ((), (), s32[]{:S(2)}) async-start(), calls=%async_computation.6 | async-start | bytes 327680 | tf_op jit(solution)/shard_map/while/body/eval_jaxpr/psum | solution.py:16
  765.2 73.7 %all-reduce.2.cloned.1.call-start = ((), (), s32[]{:S(2)}) async-start(), calls=%async_computation.6 | async-start | bytes 327680 | tf_op jit(solution)/shard_map/while/body/eval_jaxpr/psum | solution.py:16
  840.5 73.4 %all-reduce.2.cloned.1.call-start = ((), (), s32[]{:S(2)}) async-start(), calls=%async_computation.6 | async-start | bytes 327680 | tf_op jit(solution)/shard_map/while/body/eval_jaxpr/psum | solution.py:16
  915.5 73.7 %all-reduce.2.cloned.1.call-start = ((), (), s32[]{:S(2)}) async-start(), calls=%async_computation.6 | async-start | bytes 327680 | tf_op jit(solution)/shard_map/while/body/eval_jaxpr/psum | solution.py:16
  990.8 73.4 %all-reduce.2.cloned.1.call-start = ((), (), s32[]{:S(2)}) async-start(), calls=%async_computation.6 | async-start | bytes 327680 | tf_op jit(solution)/shard_map/while/body/eval_jaxpr/psum | solution.py:16
  1065.8 73.4 %all-reduce.2.cloned.1.call-start = ((), (), s32[]{:S(2)}) async-start(), calls=%async_computation.6 | async-start | bytes 327680 | tf_op jit(solution)/shard_map/while/body/eval_jaxpr/psum | solution.py:16
  1140.7 73.4 %all-reduce.2.cloned.1.call-start = ((), (), s32[]{:S(2)}) async-start(), calls=%async_computation.6 | async-start | bytes 327680 | tf_op jit(solution)/shard_map/while/body/eval_jaxpr/psum | solution.py:16
  1215.7 3.1 copy-start.5
  1215.7 4.1 copy-start.7
  1215.7 51.6 %all-gather.5.cloned.1.call-start = ((), (), s32[]{:S(2)}) async-start(), calls=%async_computation.1 | async-start | bytes 2359296 | tf_op jit(solution)/shard_map/all_gather | solution.py:115
  1216.3 100.8 %all-gather.7.cloned.1.call-start = ((), (), s32[]{:S(2)}) async-start(), calls=%async_computation.2 | async-start | bytes 2359296 | tf_op jit(solution)/shard_map/all_gather | solution.py:105
  1216.9 149.9 %all-gather.9.cloned.1.call-start = ((), (), s32[]{:S(2)}) async-start(), calls=%async_computation.3 | async-start | bytes 2359296 | tf_op jit(solution)/shard_map/all_gather | solution.py:110
  1217.5 200.4 %all-gather.11.cloned.1.call-start = ((), (), s32[]{:S(2)}) async-start(), calls=%async_computation.4 | async-start | bytes 2359296 | tf_op jit(solution)/shard_map/all_gather | solution.py:165
  1218.2 233.6 %reduce-scatter.2.cloned.1.call-start = ((), (), s32[]{:S(2)}) async-start(), calls=%async_computation.5 | async-start | bytes 2621440 | tf_op jit(solution)/shard_map/reduce_scatter | solution.py:168
  1222.9 47.4 %copy-start.2 = (bf16[512,16,2,16]{0,3,2,1:T(8,128)(2,1)}, bf16[512,16,2,16]{0,3,2,1:T(8,128)(2,1)S(1)}, u32[]{:S(2)}) copy-start(bf16[512,16,2,16]{0,3,2,1:T(8,128)(2,1)S(1)} %broadcast_select_fusion) | copy-start | bytes 1572868
  1317.0 3.1 copy-start.3
  1371.1 8.1 copy-start.4
Sparse Core Ops, SparseCore 0:
  15.1 72.1 all-reduce.1
  93.4 69.1 all-reduce.1
  168.7 69.1 all-reduce.1
  243.6 69.1 all-reduce.1
  318.6 69.1 all-reduce.1
  393.6 69.1 all-reduce.1
  468.9 69.1 all-reduce.1
  544.2 69.1 all-reduce.1
  619.5 69.1 all-reduce.1
  694.5 69.1 all-reduce.1
  769.7 69.1 all-reduce.1
  844.7 69.1 all-reduce.1
  920.0 69.1 all-reduce.1
  995.0 69.1 all-reduce.1
  1070.0 69.1 all-reduce.1
  1144.9 69.1 all-reduce.1
Sparse Core Ops, SparseCore 1:
  1218.3 49.0 all-gather.4
  1269.3 47.7 all-gather.6
  1319.0 47.7 all-gather.8
  1368.8 49.0 all-gather.10
  1422.3 29.5 reduce-scatter.1
where the time goes:
time: 1460 us
  waiting for transfers between devices  1320 us (90%)
  loops' own time  42.1 us (3%)
  local copies, waits for them, and re-layouts  35.6 us (2%)
  matrix products  32.2 us (2%)
  other arithmetic  19.2 us (1%)
  between operations  14.9 us (1%)
    psum x16, waiting for transfers between devices, spread_2(): return lax.psum(jnp.where(mine, value, jnp.zeros_like(value)), axis)  1120 us
    all_gather x1, waiting for transfers between devices, local(): lax.all_gather(key_weight, 'req', axis=0, tiled=True)  45.3 us
    all_gather x1, waiting for transfers between devices, local(): lax.all_gather(query_weight, 'req', axis=0, tiled=True)  44.6 us
    all_gather x1, waiting for transfers between devices, local(): lax.all_gather(value_weight, 'req', axis=0, tiled=True)  43.4 us
    another operation x1, loops' own time, local(): lax.fori_loop(0, active_count, fetch_one, jnp.zeros((active_count,) + sto...  42.1 us
    all_gather x1, waiting for transfers between devices, local(): lax.all_gather(output_weight, 'req', axis=1, tiled=True)  34.4 us
    reduce_scatter x1, waiting for transfers between devices, local(): lax.psum_scatter(partial_out.astype(jnp.bfloat16), 'tp', scatter_dimensio...  29.6 us
  transfers between devices with their start and end apart: 21, of which 21 were waited for; matrix products, arithmetic and copies ran while one was open for 2% of the time, Pallas kernels for 0%

commit v1 on v0

--- a/solution.py
+++ b/solution.py
@@ -11,9 +11,23 @@
 adapter_scale = 2.0
 
 
-def spread_2(value, axis, root):
-    mine = lax.axis_index(axis) == root
-    return lax.psum(jnp.where(mine, value, jnp.zeros_like(value)), axis)
+def fetch_adapters(down_part, up_part, active_slots, request_adapters, req_total):
+    slot_total = down_part.shape[0]
+    stored = jnp.concatenate([down_part, up_part], axis=1)
+    split = down_part.shape[1]
+    if slot_total * req_total <= 2 * active_slots.shape[0]:
+        fetched = lax.all_gather(stored, "req", axis=0, tiled=True)
+        places = active_slots[request_adapters]
+    else:
+        own = (active_slots // slot_total) == lax.axis_index("req")
+        rows = jnp.where(
+            own[:, None],
+            jnp.take(stored, active_slots % slot_total, axis=0),
+            jnp.zeros((), stored.dtype),
+        )
+        fetched = lax.psum(rows, "req")
+        places = request_adapters
+    return fetched[:, :split], fetched[:, split:], places
 
 
 def positions_of(segment):
@@ -77,23 +91,21 @@
     slot_total = adapter_down_weight.shape[0]
     segment = token_request_number[0]
     request_adapters = request_adapter_position[0]
-    storage_slots = jnp.take(adapter_storage_slot, adapters_in_use, axis=0)
-    stored_weight = jnp.concatenate([adapter_down_weight, adapter_up_weight], axis=3)
-
-    def fetch_one(active_index, fetched):
-        home = storage_slots[active_index]
-        own_slot = lax.dynamic_index_in_dim(stored_weight, home % slot_total, 0, keepdims=False)
-        received = spread_2(own_slot, "req", home // slot_total)
-        return lax.dynamic_update_index_in_dim(fetched, received, active_index, 0)
-
-    fetched = lax.fori_loop(
-        0,
-        active_count,
-        fetch_one,
-        jnp.zeros((active_count,) + stored_weight.shape[1:], jnp.bfloat16),
-    )
-    fetch_down = fetched[..., :model_width]
-    fetch_up = fetched[..., model_width:]
+    tp_total = lax.axis_size("tp")
+    req_total = lax.axis_size("req")
+    part_rows = reduced_rows // tp_total
+    down_part = lax.dynamic_slice_in_dim(
+        adapter_down_weight, lax.axis_index("tp") * part_rows, part_rows, 2
+    ).reshape(slot_total, 2 * part_rows * model_width)
+    up_part = adapter_up_weight.reshape(slot_total, 2 * reduced_rows * local_width)
+    down_all, up_all, request_places = fetch_adapters(
+        down_part,
+        up_part,
+        jnp.take(adapter_storage_slot, adapters_in_use, axis=0),
+        request_adapters,
+        req_total,
+    )
+    place_total = down_all.shape[0]
     floats = tokens.astype(jnp.float32)
     normed = (
         floats
@@ -117,32 +129,49 @@
     )
     request_total = request_adapters.shape[0]
     member = segment[:, None] == jnp.arange(request_total, dtype=jnp.int32)[None, :]
-    token_adapter = jnp.sum(
-        jnp.where(member, request_adapters[None, :], jnp.zeros_like(request_adapters)[None, :]),
+    token_place = jnp.sum(
+        jnp.where(member, request_places[None, :], jnp.zeros_like(request_places)[None, :]),
         axis=1,
     )
-    select = token_adapter[:, None] == jnp.arange(active_count, dtype=jnp.int32)[None, :]
+    share = 2 * part_rows
     shrunk_all = lax.dot_general(
         normed,
-        fetch_down.reshape(active_count * 2 * reduced_rows, model_width),
+        down_all.reshape(place_total * share, model_width),
         (((1,), (1,)), ((), ())),
         preferred_element_type=jnp.float32,
-    )
-    shrunk_all = shrunk_all.reshape(row_total, active_count, 2, reduced_rows)
-    shrunk = jnp.sum(
-        jnp.where(select[:, :, None, None], shrunk_all, jnp.float32(0.0)), axis=1
-    ).astype(jnp.bfloat16)
-    spread = jnp.where(select[:, :, None, None], shrunk[:, None, :, :], jnp.zeros((), jnp.bfloat16))
-    query_change = jnp.dot(
-        spread[:, :, 0, :].reshape(row_total, active_count * reduced_rows),
-        fetch_up[:, 0].reshape(active_count * reduced_rows, local_width),
-        preferred_element_type=jnp.float32,
-    )
-    value_change = jnp.dot(
-        spread[:, :, 1, :].reshape(row_total, active_count * reduced_rows),
-        fetch_up[:, 1].reshape(active_count * reduced_rows, local_width),
-        preferred_element_type=jnp.float32,
-    )
+    ).astype(jnp.bfloat16)
+    column = jnp.arange(place_total * share, dtype=jnp.int32)
+    kept = jnp.where(
+        token_place[:, None] == (column // share)[None, :], shrunk_all, jnp.zeros((), jnp.bfloat16)
+    )
+    fold = (column % share)[:, None] == jnp.arange(share, dtype=jnp.int32)[None, :]
+    shrunk_part = jnp.dot(
+        kept, fold.astype(jnp.bfloat16), preferred_element_type=jnp.float32
+    ).astype(jnp.bfloat16)
+    shrunk = lax.all_gather(shrunk_part, "tp", axis=1, tiled=True)
+    source = jnp.arange(tp_total * share, dtype=jnp.int32)
+    source_kind = (source % share) // part_rows
+    source_rank = (source // share) * part_rows + source % part_rows
+    target = jnp.arange(place_total * reduced_rows, dtype=jnp.int32)
+    mine = token_place[:, None] == (target // reduced_rows)[None, :]
+    up_all = up_all.reshape(place_total, 2, reduced_rows, local_width)
+
+    def change_of(kind):
+        spread_map = (source_kind == kind)[:, None] & (
+            source_rank[:, None] == (target % reduced_rows)[None, :]
+        )
+        spread = jnp.dot(
+            shrunk, spread_map.astype(jnp.bfloat16), preferred_element_type=jnp.float32
+        ).astype(jnp.bfloat16)
+        spread = jnp.where(mine, spread, jnp.zeros((), jnp.bfloat16))
+        return jnp.dot(
+            spread,
+            up_all[:, kind].reshape(place_total * reduced_rows, local_width),
+            preferred_element_type=jnp.float32,
+        )
+
+    query_change = change_of(0)
+    value_change = change_of(1)
     head_total = local_width // HEAD_WIDTH
     token_positions = positions_of(segment)
     query_per_head = apply_rotation(

time: 1460 us -> 297 us (0.20)
  waiting for transfers between devices: 1320 us -> 228 us
  loops' own time: 42.1 us -> 0 us
  local copies, waits for them, and re-layouts: 35.6 us -> 7.27 us
    psum x16 -> x0, waiting for transfers between devices: 1120 us -> none  [spread_2(): return lax.psum(jnp.where(mine, value, jnp.zeros_like(value)), axis)]
    another operation x1 -> x0, loops' own time: 42.1 us -> none  [local(): lax.fori_loop(0, active_count, fetch_one, jnp.zeros((active_count,) + sto...]
    all_gather x0 -> x1, waiting for transfers between devices: none -> 33.5 us  [fetch_adapters(): fetched = lax.all_gather(stored, 'req', axis=0, tiled=True)]
    dynamic_update_slice x16 -> x0, local copies, waits for them, and re-layouts: 25.4 us -> none  [fetch_one(): return lax.dynamic_update_index_in_dim(fetched, received, active_index, 0)]
  transfers between devices with their start and end apart: 21 -> 6, of which waited for: 21 -> 6; matrix products, arithmetic and copies ran while one was open for 2% -> 14% of each run, Pallas kernels for 0% -> 0%
where the time goes in v1:
time: 297 us
  waiting for transfers between devices  228 us (77%)
  matrix products  31.7 us (11%)
  between operations  13.7 us (5%)
  other arithmetic  10.1 us (3%)
  local copies, waits for them, and re-layouts  7.27 us (2%)
  blocking collectives  5.39 us (2%)
    all_gather x1, waiting for transfers between devices, local(): lax.all_gather(query_weight, 'req', axis=0, tiled=True)  44.7 us
    all_gather x1, waiting for transfers between devices, local(): lax.all_gather(key_weight, 'req', axis=0, tiled=True)  44 us
    all_gather x1, waiting for transfers between devices, local(): lax.all_gather(value_weight, 'req', axis=0, tiled=True)  39.2 us
    all_gather x1, waiting for transfers between devices, local(): lax.all_gather(output_weight, 'req', axis=1, tiled=True)  34.7 us
    all_gather x1, waiting for transfers between devices, fetch_adapters(): fetched = lax.all_gather(stored, 'req', axis=0, tiled=True)  33.5 us
    reduce_scatter x1, waiting for transfers between devices, local(): lax.psum_scatter(partial_out.astype(jnp.bfloat16), 'tp', scatter_dimensio...  29.8 us
    sub x1, matrix products, attend(): scores - row_peak  8.2 us
  transfers between devices with their start and end apart: 6, of which 6 were waited for; matrix products, arithmetic and copies ran while one was open for 14% of the time, Pallas kernels for 0%

profile of v1, /device:TPU:0, one launch (start us, length us, event | category | flops | bytes accessed | tf_op | source)
XLA Modules:
  0.0 296.7 jit_solution(14154784594400048160)
XLA Ops:
  6.5 0.0 all-gather.15.cloned.1.call-start
  6.6 1.0 copy.18
  7.7 0.1 reshape.292
  7.7 0.8 maximum_bitcast_fusion
  8.5 0.0 all-gather.7.cloned.1.call-start
  8.6 0.7 all-gather.7.cloned.1.call-update
  9.3 0.7 all-gather.9.cloned.1.call-update
  10.1 0.5 all-gather.11.cloned.1.call-update
  10.6 0.0 all-gather.13.cloned.1.call-start
  10.6 0.5 all-gather.13.cloned.1.call-update
  11.2 0.0 reduce-scatter.2.cloned.1.call-start
  11.3 0.7 convert_element_type.59
  12.0 2.1 fusion.2
  14.1 0.7 compare_select_fusion.1
  14.8 0.7 gather_fusion
  15.5 0.1 compare_reduce_fusion
  15.6 0.9 fusion.18
  16.5 0.6 gather_fusion.1
  17.1 0.1 select_reduce_fusion
  17.2 0.1 add_select_fusion
  17.3 0.3 reduce-window.9
  17.6 0.1 slice.46
  17.7 0.1 slice_reduce_fusion
  17.8 0.1 fusion.47
  17.9 0.9 multiply_cosine_fusion
  18.9 33.5 %all-gather.15.cloned.1.call-done = bf16[8,2,32768]{2,1,0:T(2,128)(2,1)} async-done(((bf16[1,2,32768]{2,1,0:T(2,128)(2,1)}), bf16[8,2,32768]{2,1,0:T(2,128)(2,1)}) %all-gather.15.cloned.1.call-update) | async-done | bytes 1048592 | tf_op jit(solution)/shard_map/all_gather | solution.py:19
  52.4 1.5 reshape.319
  53.9 0.9 fusion.70
  54.7 0.2 copy.19
  54.9 0.9 fusion.71
  55.8 1.3 reshape.294
  57.0 0.9 fusion.17
  58.0 5.4 %all_gather.20 = bf16[512,32]{0,1:T(8,128)(2,1)S(1)} all-gather(bf16[512,8]{0,1:T(8,128)(2,1)S(1)} %fusion.17), channel_id=1, replica_groups=mesh['req'=8,'tp'=4] {'tp'}, dimensions={1}, use_global_device_ids=true | all-gather | bytes 40960 | tf_op jit(solution)/shard_map/all_gather | solution.py:151
  63.4 39.2 %all-gather.7.cloned.1.call-done = bf16[2048,512]{1,0:T(8,128)(2,1)} async-done(((bf16[256,512]{1,0:T(8,128)(2,1)}), bf16[2048,512]{1,0:T(8,128)(2,1)}) %all-gather.7.cloned.1.call-update) | async-done | bytes 2097168 | tf_op jit(solution)/shard_map/all_gather | solution.py:127
  102.6 3.0 %fusion.68 = f32[512,512]{0,1:T(8,128)S(1)} fusion(bf16[2048,512]{1,0:T(8,128)(2,1)} %all-gather.7.cloned.1.call-done, bf16[512,2048]{1,0:T(8,128)(2,1)S(1)} %copy-done.2, f32[2048]{0:T(1024)S(1)} %convert_element_type.59, f32[512]{0:T(512)S(1)} %add_rsqrt_fusion), kind=kOutput, calls=%fused_computation.120 | convolution fusion | flops 1077936128 | bytes 5253120 | tf_op jit(solution)/shard_map/dot_general | solution.py:125
  105.6 2.3 fusion.12
  107.9 44.7 %all-gather.9.cloned.1.call-done = bf16[2048,512]{1,0:T(8,128)(2,1)} async-done(((bf16[256,512]{1,0:T(8,128)(2,1)}), bf16[2048,512]{1,0:T(8,128)(2,1)}) %all-gather.9.cloned.1.call-update) | async-done | bytes 2097168 | tf_op jit(solution)/shard_map/all_gather | solution.py:117
  152.5 3.9 %fusion.64 = f32[512,512]{0,1:T(8,128)} fusion(bf16[2048,512]{1,0:T(8,128)(2,1)} %all-gather.9.cloned.1.call-done, bf16[512,2048]{1,0:T(8,128)(2,1)S(1)} %copy-done.2, f32[2048]{0:T(1024)S(1)} %convert_element_type.59, f32[512]{0:T(512)S(1)} %add_rsqrt_fusion), kind=kOutput, calls=%fused_computation.119 | convolution fusion | flops 1077936128 | bytes 5253120 | tf_op jit(solution)/shard_map/dot_general | solution.py:115
  156.5 1.9 fusion.9
  158.4 44.0 %all-gather.11.cloned.1.call-done = bf16[2048,512]{1,0:T(8,128)(2,1)} async-done(((bf16[256,512]{1,0:T(8,128)(2,1)}), bf16[2048,512]{1,0:T(8,128)(2,1)}) %all-gather.11.cloned.1.call-update) | async-done | bytes 2097168 | tf_op jit(solution)/shard_map/all_gather | solution.py:122
  202.3 3.0 %fusion.62 = f32[512,512]{0,1:T(8,128)S(1)} fusion(bf16[2048,512]{1,0:T(8,128)(2,1)} %all-gather.11.cloned.1.call-done, bf16[512,2048]{1,0:T(8,128)(2,1)S(1)} %copy-done.2, f32[2048]{0:T(1024)S(1)} %convert_element_type.59, f32[512]{0:T(512)S(1)} %add_rsqrt_fusion), kind=kOutput, calls=%fused_computation.118 | convolution fusion | flops 1077936128 | bytes 5253120 | tf_op jit(solution)/shard_map/dot_general | solution.py:120
  205.4 1.3 subtract_convert_fusion.1
  206.7 8.2 %fusion.72 = (f32[8,512]{1,0:T(8,128)S(1)}, f32[8,512,512]{1,2,0:T(8,128)}) fusion(pred[512,512]{0,1:T(8,128)(4,1)} %fusion.18, bf16[512,8,32]{0,2,1:T(8,128)(2,1)} %get-tuple-element.13, bf16[512,8,32]{0,2,1:T(8,128)(2,1)} %get-tuple-element.14, bf16[512,8,32]{0,2,1:T(8,128)(2,1)} %get-tuple-element.6, bf16[512,8,32]{0,2,1:T(8,128)(2,1)} %get-tuple-element.5), kind=kOutput, calls=%fused_computation.123 | convolution fusion | flops 281018880 | bytes 9715712 | tf_op jit(solution)/shard_map/sub | solution.py:66
  214.9 4.3 %fusion.11 = bf16[8,64,512]{2,1,0:T(8,128)(2,1)S(1)} fusion(bf16[512,8,64]{0,2,1:T(8,128)(2,1)S(1)} %bitcast.46, f32[8,512,512]{1,2,0:T(8,128)} %get-tuple-element.18, f32[8,512]{1,0:T(8,128)S(1)} %get-tuple-element.17), kind=kOutput, calls=%fused_computation.21 | convolution fusion | flops 272891904 | bytes 9453568 | tf_op jit(solution)/shard_map/hqk,khd->qhd/dot_general | solution.py:68
  219.2 34.7 %all-gather.13.cloned.1.call-done = bf16[512,2048]{1,0:T(8,128)(2,1)} async-done(((bf16[512,256]{1,0:T(8,128)(2,1)}), bf16[512,2048]{1,0:T(8,128)(2,1)}) %all-gather.13.cloned.1.call-update) | async-done | bytes 2097168 | tf_op jit(solution)/shard_map/all_gather | solution.py:194
  253.8 4.2 %convolution_convert_fusion = bf16[512,2048]{1,0:T(8,128)(2,1)} fusion(bf16[512,512]{0,1:T(8,128)(2,1)S(1)} %bitcast.51, bf16[512,2048]{1,0:T(8,128)(2,1)} %all-gather.13.cloned.1.call-done), kind=kOutput, calls=%fused_computation.16 | convolution fusion | flops 1074790400 | bytes 4718592 | tf_op jit(solution)/shard_map/dot_general | solution.py:192
  258.1 29.8 %reduce-scatter.2.cloned.1.call-done = bf16[512,512]{1,0:T(8,128)(2,1)} async-done(((bf16[512,2048]{1,0:T(8,128)(2,1)}), bf16[512,512]{1,0:T(8,128)(2,1)}) %reduce-scatter.2.cloned.1.call-update) | async-done | bytes 524304 | tf_op jit(solution)/shard_map/reduce_scatter | solution.py:197
  287.8 2.0 add_convert_fusion
  (33 shorter events, 0.3 us)
Async XLA Ops:
  6.5 1.1 copy-start
  6.5 8.9 %copy-start.6 = (s32[16]{0:T(128)S(1)}, s32[16]{0:T(128)}, u32[]{:S(2)}) copy-start(s32[16]{0:T(128)} %param.15) | copy-start | bytes 196
  6.5 8.2 %copy-start.1 = (s32[16]{0:T(128)S(1)}, s32[16]{0:T(128)}, u32[]{:S(2)}) copy-start(s32[16]{0:T(128)} %param.16) | copy-start | bytes 196
  6.5 8.9 %copy-start.7 = (s32[1,8]{1,0:T(1,128)S(1)}, s32[1,8]{1,0:T(1,128)}, u32[]{:S(2)}) copy-start(s32[1,8]{1,0:T(1,128)} %param.14) | copy-start | bytes 100
  6.5 8.9 %copy-start.5 = (s32[1,512]{1,0:T(1,128)S(1)}, s32[1,512]{1,0:T(1,128)}, u32[]{:S(2)}) copy-start(s32[1,512]{1,0:T(1,128)} %param.13) | copy-start | bytes 6148
  6.5 45.8 %all-gather.15.cloned.1.call-start = ((), (), s32[]{:S(2)}) async-start(), calls=%async_computation.6 | async-start | bytes 1179648 | tf_op jit(solution)/shard_map/all_gather | solution.py:19
  8.5 94.1 %all-gather.7.cloned.1.call-start = ((), (), s32[]{:S(2)}) async-start(), calls=%async_computation.1 | async-start | bytes 2359296 | tf_op jit(solution)/shard_map/all_gather | solution.py:127
  9.3 143.3 %all-gather.9.cloned.1.call-start = ((), (), s32[]{:S(2)}) async-start(), calls=%async_computation.2 | async-start | bytes 2359296 | tf_op jit(solution)/shard_map/all_gather | solution.py:117
  10.0 192.3 %all-gather.11.cloned.1.call-start = ((), (), s32[]{:S(2)}) async-start(), calls=%async_computation.3 | async-start | bytes 2359296 | tf_op jit(solution)/shard_map/all_gather | solution.py:122
  10.6 243.2 %all-gather.13.cloned.1.call-start = ((), (), s32[]{:S(2)}) async-start(), calls=%async_computation.4 | async-start | bytes 2359296 | tf_op jit(solution)/shard_map/all_gather | solution.py:194
  11.2 276.6 %reduce-scatter.2.cloned.1.call-start = ((), (), s32[]{:S(2)}) async-start(), calls=%async_computation.5 | async-start | bytes 2621440 | tf_op jit(solution)/shard_map/reduce_scatter | solution.py:197
  15.4 41.6 %copy-start.2 = (bf16[512,2048]{1,0:T(8,128)(2,1)S(1)}, bf16[512,2048]{1,0:T(8,128)(2,1)}, u32[]{:S(2)}) copy-start(bf16[512,2048]{1,0:T(8,128)(2,1)} %param.12) | copy-start | bytes 6291460
  202.3 3.0 %copy-start.4 = (f32[512,32]{0,1:T(8,128)S(1)}, f32[512,32]{0,1:T(8,128)}, u32[]{:S(2)}) copy-start(f32[512,32]{0,1:T(8,128)} %get-tuple-element.16) | copy-start | bytes 196612
  206.7 8.2 %copy-start.3 = (bf16[512,512]{0,1:T(8,128)(2,1)S(1)}, bf16[512,512]{0,1:T(8,128)(2,1)}, u32[]{:S(2)}) copy-start(bf16[512,512]{0,1:T(8,128)(2,1)} %fusion.12) | copy-start | bytes 1572868
Sparse Core Ops, SparseCore 0:
  9.5 42.8 all-gather.14
  54.5 48.0 all-gather.6
  104.7 47.7 all-gather.8
  154.5 47.7 all-gather.10
  204.2 49.5 all-gather.12
  258.2 29.5 reduce-scatter.1

commit v2 on v1

--- a/solution.py
+++ b/solution.py
@@ -1,6 +1,10 @@
+import functools
+
 import jax
 import jax.numpy as jnp
 from jax import lax
+from jax.experimental import pallas as pl
+from jax.experimental.pallas import tpu as pltpu
 from jax.sharding import PartitionSpec as P
 
 HEAD_WIDTH = 64
@@ -11,23 +15,143 @@
 adapter_scale = 2.0
 
 
-def fetch_adapters(down_part, up_part, active_slots, request_adapters, req_total):
-    slot_total = down_part.shape[0]
-    stored = jnp.concatenate([down_part, up_part], axis=1)
-    split = down_part.shape[1]
-    if slot_total * req_total <= 2 * active_slots.shape[0]:
-        fetched = lax.all_gather(stored, "req", axis=0, tiled=True)
-        places = active_slots[request_adapters]
+def relay_kernel(lines, axes, *refs):
+    count = len(axes)
+    sources, gathered = refs[:count], refs[count : 2 * count]
+    send_sems, recv_sems, local_sems = refs[2 * count :]
+    me = lax.axis_index("req")
+    line = lax.div(me, 2)
+    side = lax.rem(me, 2)
+    partner = 2 * line + 1 - side
+    has_up = line < lines - 1
+    has_down = line > 0
+
+    def block(index, origin):
+        if axes[index] == 0:
+            return gathered[index].at[origin]
+        width = sources[index].shape[1]
+        return gathered[index].at[:, pl.ds(pl.multiple_of(origin * width, width), width)]
+
+    def to_device(index, origin, slot, target):
+        source = sources[index] if slot < 3 else block(index, origin)
+        return pltpu.make_async_remote_copy(
+            src_ref=source,
+            dst_ref=block(index, origin),
+            send_sem=send_sems.at[index, slot],
+            recv_sem=recv_sems.at[index, origin],
+            device_id={"req": target},
+            device_id_type=pl.DeviceIdType.MESH,
+        )
+
+    def arrival(index, origin):
+        to_device(index, origin, 3, partner).wait_recv()
+
+    barrier = pltpu.get_barrier_semaphore()
+
+    def greet(target):
+        pl.semaphore_signal(
+            barrier, inc=1, device_id={"req": target}, device_id_type=pl.DeviceIdType.MESH
+        )
+
+    greet(partner)
+    pl.when(has_up)(lambda: greet(me + 2))
+    pl.when(has_down)(lambda: greet(me - 2))
+    pl.semaphore_wait(barrier, 1 + has_up.astype(jnp.int32) + has_down.astype(jnp.int32))
+
+    for index in range(count):
+        pl.when(has_up)(lambda: to_device(index, me, 0, me + 2).start())
+        pl.when(has_down)(lambda: to_device(index, me, 1, me - 2).start())
+        to_device(index, me, 2, partner).start()
+    for index in range(count):
+        pltpu.make_async_copy(sources[index], block(index, me), local_sems.at[index]).start()
+    for step in range(1, lines):
+        slot = 3 + 4 * (step - 1)
+        for index in range(count):
+
+            @pl.when(line >= step)
+            def _():
+                origin = me - 2 * step
+                arrival(index, origin)
+                pl.when(has_up)(lambda: to_device(index, origin, slot, me + 2).start())
+                to_device(index, origin, slot + 1, partner).start()
+
+            @pl.when(line + step < lines)
+            def _():
+                origin = me + 2 * step
+                arrival(index, origin)
+                pl.when(has_down)(lambda: to_device(index, origin, slot + 2, me - 2).start())
+                to_device(index, origin, slot + 3, partner).start()
+
+    for index in range(count):
+        for other in range(lines):
+            arrival(index, 2 * other + 1 - side)
+        pltpu.make_async_copy(sources[index], block(index, me), local_sems.at[index]).wait()
+        pl.when(has_up)(lambda: to_device(index, me, 0, me + 2).wait_send())
+        pl.when(has_down)(lambda: to_device(index, me, 1, me - 2).wait_send())
+        to_device(index, me, 2, partner).wait_send()
+        for step in range(1, lines):
+            slot = 3 + 4 * (step - 1)
+
+            @pl.when(line >= step)
+            def _():
+                origin = me - 2 * step
+                pl.when(has_up)(lambda: to_device(index, origin, slot, me + 2).wait_send())
+                to_device(index, origin, slot + 1, partner).wait_send()
+
+            @pl.when(line + step < lines)
+            def _():
+                origin = me + 2 * step
+                pl.when(has_down)(lambda: to_device(index, origin, slot + 2, me - 2).wait_send())
+                to_device(index, origin, slot + 3, partner).wait_send()
+
+
+def relay_gather(arrays, axes, req_total):
+    lines = req_total // 2
+    count = len(arrays)
+    shapes = []
+    for array, axis in zip(arrays, axes):
+        if axis == 0:
+            shape = (req_total,) + array.shape
+        else:
+            shape = (array.shape[0], req_total * array.shape[1])
+        shapes.append(jax.ShapeDtypeStruct(shape, array.dtype))
+    return pl.pallas_call(
+        functools.partial(relay_kernel, lines, tuple(axes)),
+        out_shape=shapes,
+        in_specs=[pl.BlockSpec(memory_space=pl.ANY)] * count,
+        out_specs=[pl.BlockSpec(memory_space=pl.ANY)] * count,
+        scratch_shapes=[
+            pltpu.SemaphoreType.DMA((count, 3 + 4 * (lines - 1))),
+            pltpu.SemaphoreType.DMA((count, req_total)),
+            pltpu.SemaphoreType.DMA((count,)),
+        ],
+        compiler_params=pltpu.CompilerParams(collective_id=0, has_side_effects=True),
+    )(*arrays)
+
+
+def gather_all(arrays, axes, req_total):
+    if req_total % 2 == 0 and req_total <= 16:
+        gathered = relay_gather(arrays, axes, req_total)
     else:
-        own = (active_slots // slot_total) == lax.axis_index("req")
-        rows = jnp.where(
-            own[:, None],
-            jnp.take(stored, active_slots % slot_total, axis=0),
-            jnp.zeros((), stored.dtype),
-        )
-        fetched = lax.psum(rows, "req")
-        places = request_adapters
-    return fetched[:, :split], fetched[:, split:], places
+        gathered = [
+            lax.all_gather(array, "req", axis=axis, tiled=axis == 1)
+            for array, axis in zip(arrays, axes)
+        ]
+    return [
+        array.reshape((-1,) + array.shape[2:]) if axis == 0 else array
+        for array, axis in zip(gathered, axes)
+    ]
+
+
+def active_rows(stored, active_slots):
+    slot_total = stored.shape[0]
+    own = (active_slots // slot_total) == lax.axis_index("req")
+    rows = jnp.where(
+        own[:, None, None],
+        jnp.take(stored, active_slots % slot_total, axis=0),
+        jnp.zeros((), stored.dtype),
+    )
+    return lax.psum(rows, "req").reshape(-1, stored.shape[2])
 
 
 def positions_of(segment):
@@ -87,25 +211,35 @@
     row_total, model_width = tokens.shape
     local_width = query_weight.shape[1]
     reduced_rows = adapter_down_weight.shape[2]
-    active_count = adapters_in_use.shape[0]
     slot_total = adapter_down_weight.shape[0]
     segment = token_request_number[0]
     request_adapters = request_adapter_position[0]
     tp_total = lax.axis_size("tp")
     req_total = lax.axis_size("req")
     part_rows = reduced_rows // tp_total
+    share = 2 * part_rows
     down_part = lax.dynamic_slice_in_dim(
         adapter_down_weight, lax.axis_index("tp") * part_rows, part_rows, 2
-    ).reshape(slot_total, 2 * part_rows * model_width)
-    up_part = adapter_up_weight.reshape(slot_total, 2 * reduced_rows * local_width)
-    down_all, up_all, request_places = fetch_adapters(
-        down_part,
-        up_part,
-        jnp.take(adapter_storage_slot, adapters_in_use, axis=0),
-        request_adapters,
-        req_total,
-    )
-    place_total = down_all.shape[0]
+    ).reshape(slot_total, share, model_width)
+    up_part = adapter_up_weight.reshape(slot_total, 2 * reduced_rows, local_width)
+    active_slots = jnp.take(adapter_storage_slot, adapters_in_use, axis=0)
+    arrays = [query_weight, key_weight, value_weight, output_weight]
+    axes = [0, 0, 0, 1]
+    if slot_total * req_total <= 2 * active_slots.shape[0]:
+        adapter_parts = [
+            down_part.reshape(slot_total * share, model_width),
+            up_part.reshape(slot_total * 2 * reduced_rows, local_width),
+        ]
+        down_all, up_all, query_full, key_full, value_full, output_full = gather_all(
+            adapter_parts + arrays, [0, 0] + axes, req_total
+        )
+        request_places = active_slots[request_adapters]
+    else:
+        down_all = active_rows(down_part, active_slots)
+        up_all = active_rows(up_part, active_slots)
+        query_full, key_full, value_full, output_full = gather_all(arrays, axes, req_total)
+        request_places = request_adapters
+    place_total = down_all.shape[0] // share
     floats = tokens.astype(jnp.float32)
     normed = (
         floats
@@ -114,17 +248,17 @@
     ).astype(jnp.bfloat16)
     query_plain = jnp.dot(
         normed,
-        lax.all_gather(query_weight, "req", axis=0, tiled=True),
+        query_full,
         preferred_element_type=jnp.float32,
     )
     key_base = jnp.dot(
         normed,
-        lax.all_gather(key_weight, "req", axis=0, tiled=True),
+        key_full,
         preferred_element_type=jnp.float32,
     )
     value_plain = jnp.dot(
         normed,
-        lax.all_gather(value_weight, "req", axis=0, tiled=True),
+        value_full,
         preferred_element_type=jnp.float32,
     )
     request_total = request_adapters.shape[0]
@@ -133,10 +267,9 @@
         jnp.where(member, request_places[None, :], jnp.zeros_like(request_places)[None, :]),
         axis=1,
     )
-    share = 2 * part_rows
     shrunk_all = lax.dot_general(
         normed,
-        down_all.reshape(place_total * share, model_width),
+        down_all,
         (((1,), (1,)), ((), ())),
         preferred_element_type=jnp.float32,
     ).astype(jnp.bfloat16)
@@ -191,7 +324,7 @@
     )
     partial_out = jnp.dot(
         attended,
-        lax.all_gather(output_weight, "req", axis=1, tiled=True),
+        output_full,
         preferred_element_type=jnp.float32,
     )
     summed = lax.psum_scatter(

time: 297 us -> 214 us (0.72)
  waiting for transfers between devices: 228 us -> 31.8 us
  Pallas kernels: 0 us -> 108 us
  other arithmetic: 10.1 us -> 14.2 us
    all_gather x5 -> x0, waiting for transfers between devices: 196 us -> none  [the longest x1 44.7 us: local(): lax.all_gather(query_weight, 'req', axis=0, tiled=True)]
    pallas_call x0 -> x1, Pallas kernels: none -> 108 us  [relay_gather(): pl.pallas_call(functools.partial(relay_kernel, lines, tuple(axes)), out_s...]
    dot_general x0 -> x1, local copies, waits for them, and re-layouts: none -> 3.97 us  [local(): key_base = jnp.dot(normed, key_full, preferred_element_type=jnp.float32)]
  transfers between devices with their start and end apart: 6 -> 1, of which waited for: 6 -> 1; matrix products, arithmetic and copies ran while one was open for 14% -> 0% of each run, Pallas kernels for 0% -> 0%
where the time goes in v2:
time: 214 us
  Pallas kernels  108 us (50%)
  matrix products  32.2 us (15%)
  waiting for transfers between devices  31.8 us (15%)
  other arithmetic  14.2 us (7%)
  between operations  13.5 us (6%)
  local copies, waits for them, and re-layouts  8.7 us (4%)
  blocking collectives  5.39 us (3%)
    pallas_call x1, Pallas kernels, relay_gather(): pl.pallas_call(functools.partial(relay_kernel, lines, tuple(axes)), out_s...  108 us
    reduce_scatter x1, waiting for transfers between devices, local(): lax.psum_scatter(partial_out.astype(jnp.bfloat16), 'tp', scatter_dimensio...  31.8 us
    sub x1, matrix products, attend(): scores - row_peak  8.2 us
    all_gather x1, blocking collectives, local(): shrunk = lax.all_gather(shrunk_part, 'tp', axis=1, tiled=True)  5.39 us
    dot_general x1, matrix products, attend(): jnp.einsum('hqk,khd->qhd', weights, value_per_head, preferred_element_typ...  4.38 us
  transfers between devices with their start and end apart: 1, of which 1 were waited for; matrix products, arithmetic and copies ran while one was open for 0% of the time, Pallas kernels for 0%

profile of v2, /device:TPU:0, one launch (start us, length us, event | category | flops | bytes accessed | tf_op | source)
XLA Modules:
  0.0 213.6 jit_solution(9567142418902278529)
XLA Ops:
  6.5 0.0 copy-start
  6.5 0.0 copy-start.1
  6.5 0.0 reduce-scatter.2.cloned.1.call-start
  6.6 0.8 fusion.54
  7.4 0.8 compare_reduce_fusion
  8.3 0.7 compare_select_fusion.1
  8.9 0.1 add_select_fusion
  9.0 0.3 reduce-window.9
  9.3 0.1 slice.38
  9.4 0.1 slice_reduce_fusion
  9.5 0.1 fusion.49
  9.6 2.1 fusion.2
  11.7 1.3 gather_fusion
  13.0 0.7 and_select_fusion.8
  13.7 1.7 fusion.20
  15.4 0.6 gather_fusion.1
  16.0 0.8 select_reduce_fusion
  16.8 0.7 convert_element_type.59
  17.5 0.0 copy-done
  17.5 0.7 reshape_reshape.9.refs_0_
  18.2 107.7 %shard_map.118 = (bf16[8,16,2048]{2,1,0:T(8,128)(2,1)}, bf16[8,64,512]{2,1,0:T(8,128)(2,1)}, bf16[8,256,512]{2,1,0:T(8,128)(2,1)}, bf16[8,256,512]{2,1,0:T(8,128...) custom-call(bf16[16,2048]{1,0:T(8,128)(2,1)} %reshape_reshape.9.refs_0_, bf16[64,512]{1,0:T(8,128)(2,1)} %bitcast.50, ...), custom_call_target="tpu_custom_call" | custom-call | tf_op jit(solution)/shard_map/pallas_call | solution.py:118
  125.9 0.0 copy-done.1
  125.9 3.0 %fusion.69 = f32[512,512]{0,1:T(8,128)S(1)} fusion(bf16[2048,512]{1,0:T(8,128)(2,1)} %bitcast.54, bf16[512,2048]{1,0:T(8,128)(2,1)S(1)} %copy-done.1, f32[2048]{0:T(1024)S(1)} %convert_element_type.59, f32[512]{0:T(512)S(1)} %add_rsqrt_fusion), kind=kOutput, calls=%fused_computation.120 | convolution fusion | flops 1077936128 | bytes 5253120 | tf_op jit(solution)/shard_map/dot_general | solution.py:259
  128.9 2.0 fusion.19
  130.9 5.4 %all_gather.3 = bf16[512,32]{0,1:T(8,128)(2,1)S(1)} all-gather(bf16[512,8]{0,1:T(8,128)(2,1)S(1)} %fusion.19), channel_id=1, replica_groups=mesh['req'=8,'tp'=4] {'tp'}, dimensions={1}, use_global_device_ids=true | all-gather | bytes 40960 | tf_op jit(solution)/shard_map/all_gather | solution.py:284
  136.2 1.9 fusion.71
  138.1 4.0 %fusion.65 = f32[512,512]{0,1:T(8,128)} fusion(bf16[2048,512]{1,0:T(8,128)(2,1)} %bitcast.53, bf16[512,2048]{1,0:T(8,128)(2,1)S(1)} %copy-done.1, f32[2048]{0:T(1024)S(1)} %convert_element_type.59, f32[512]{0:T(512)S(1)} %add_rsqrt_fusion), kind=kOutput, calls=%fused_computation.119 | convolution fusion | flops 1077936128 | bytes 5253120 | tf_op jit(solution)/shard_map/dot_general | solution.py:249
  142.1 4.0 %copy.17 = bf16[512,2048]{1,0:T(8,128)(2,1)} copy(bf16[512,2048]{0,1:T(8,128)(2,1)} %bitcast.44) | data formatting | bytes 4194304 | tf_op jit(solution)/shard_map/dot_general | solution.py:254
  146.0 3.9 %fusion.9 = f32[512,8,64]{0,2,1:T(8,128)} fusion(bf16[8,64,2048]{2,1,0:T(8,128)(2,1)} %bitcast.45, bf16[512,2048]{1,0:T(8,128)(2,1)S(1)} %copy-done.1, f32[2048]{0:T(1024)S(1)} %convert_element_type.59, f32[512]{0:T(512)S(1)} %add_rsqrt_fusion), kind=kOutput, calls=%fused_computation.17 | convolution fusion | flops 1077936128 | bytes 5253120 | tf_op jit(solution)/shard_map/dot_general | solution.py:254
  150.0 0.9 multiply_cosine_fusion
  150.9 2.3 %fusion.14 = bf16[512,512]{0,1:T(8,128)(2,1)} fusion(f32[512,512]{0,1:T(8,128)S(1)} %fusion.69, bf16[256,512]{1,0:T(8,128)(2,1)} %bitcast.47, bf16[512,32]{0,1:T(8,128)(2,1)S(1)} %all_gather.3, s32[256]{0:T(256)S(1)} %get-tuple-element.34, s32[512]{0:T(512)S(1)} %select_reduce_fusion, s32[256]{0:T(256)S(1)} %get-tuple-element.33, s32[32]{0:T(128)S(1)} %fusion.52, ...), kind=kOutput, calls=%fused_computation.24 | convolution fusion | flops 143802368 | bytes 1872032 | tf_op jit(solution)/shard_map/dot_general | solution.py:300
  153.2 1.9 fusion.11
  155.1 2.6 %subtract_convert_fusion.1 = (bf16[512,8,32]{0,2,1:T(8,128)(2,1)}, bf16[512,8,32]{0,2,1:T(8,128)(2,1)}, bf16[512,8,32]{0,2,1:T(8,128)(2,1)}, bf16[512,8,32]{0,2,1:T(8,128)(2,1)}) fusion(f32[512,8,64]{0,2,1:T(8,128)S(1)} %bitcast.43, f32[512,32]{0,1:T(8,128)} %get-tuple-element.26, f32[512,32]{0,1:T(8,128)S(1)} %get-tuple-element.25, f32[512,8,64]{0,2,1:T(8,128)} %fusion.9), kind=kLoop, calls=%fused_computation.44 | loop fusion | flops 2097152 | bytes 3276800 | tf_op jit(solution)/shard_map/convert.2
  157.7 0.0 copy-start.2
  157.7 8.2 %fusion.72 = (f32[8,512]{1,0:T(8,128)S(1)}, f32[8,512,512]{1,2,0:T(8,128)}) fusion(pred[512,512]{0,1:T(8,128)(4,1)} %fusion.20, bf16[512,8,32]{0,2,1:T(8,128)(2,1)} %get-tuple-element.23, bf16[512,8,32]{0,2,1:T(8,128)(2,1)} %get-tuple-element.24, bf16[512,8,32]{0,2,1:T(8,128)(2,1)} %get-tuple-element.18, bf16[512,8,32]{0,2,1:T(8,128)(2,1)} %get-tuple-element.17), kind=kOutput, calls=%fused_computation.122 | convolution fusion | flops 281018880 | bytes 9715712 | tf_op jit(solution)/shard_map/sub | solution.py:190
  165.9 0.0 copy-done.2
  165.9 0.0 copy-start.3
  165.9 4.4 %fusion.13 = bf16[8,64,512]{2,1,0:T(8,128)(2,1)S(1)} fusion(bf16[512,8,64]{0,2,1:T(8,128)(2,1)S(1)} %bitcast.48, f32[8,512,512]{1,2,0:T(8,128)} %get-tuple-element.28, f32[8,512]{1,0:T(8,128)S(1)} %get-tuple-element.27), kind=kOutput, calls=%fused_computation.23 | convolution fusion | flops 272891904 | bytes 9453568 | tf_op jit(solution)/shard_map/hqk,khd->qhd/dot_general | solution.py:192
  170.3 0.0 copy-done.3
  170.3 2.6 %convolution_convert_fusion = bf16[512,2048]{1,0:T(8,128)(2,1)} fusion(bf16[512,512]{0,1:T(8,128)(2,1)S(1)} %bitcast.56, bf16[512,2048]{1,0:T(8,128)(2,1)S(1)} %copy-done.3), kind=kOutput, calls=%fused_computation.16 | convolution fusion | flops 1074790400 | bytes 4718592 | tf_op jit(solution)/shard_map/dot_general | solution.py:325
  172.9 0.0 reduce-scatter.2.cloned.1.call-update
  173.0 31.8 %reduce-scatter.2.cloned.1.call-done = bf16[512,512]{1,0:T(8,128)(2,1)} async-done(((bf16[512,2048]{1,0:T(8,128)(2,1)}), bf16[512,512]{1,0:T(8,128)(2,1)}) %reduce-scatter.2.cloned.1.call-update) | async-done | bytes 524304 | tf_op jit(solution)/shard_map/reduce_scatter | solution.py:330
  204.7 2.0 add_convert_fusion
  (10 shorter events, 0.1 us)
Async XLA Ops:
  6.5 11.0 %copy-start = (bf16[2,2,16,2048]{3,2,1,0:T(8,128)(2,1)S(1)}, bf16[2,2,16,2048]{3,2,1,0:T(8,128)(2,1)}, u32[]{:S(2)}) copy-start(bf16[2,2,16,2048]{3,2,1,0:T(8,128)(2,1)} %param.22) | copy-start | bytes 786436
  6.5 119.4 %copy-start.1 = (bf16[512,2048]{1,0:T(8,128)(2,1)S(1)}, bf16[512,2048]{1,0:T(8,128)(2,1)}, u32[]{:S(2)}) copy-start(bf16[512,2048]{1,0:T(8,128)(2,1)} %param.12) | copy-start | bytes 6291460
  6.5 198.2 %reduce-scatter.2.cloned.1.call-start = ((), (), s32[]{:S(2)}) async-start(), calls=%async_computation.1 | async-start | bytes 2621440 | tf_op jit(solution)/shard_map/reduce_scatter | solution.py:330
  157.7 8.2 %copy-start.2 = (bf16[512,512]{0,1:T(8,128)(2,1)S(1)}, bf16[512,512]{0,1:T(8,128)(2,1)}, u32[]{:S(2)}) copy-start(bf16[512,512]{0,1:T(8,128)(2,1)} %fusion.14) | copy-start | bytes 1572868
  165.9 4.4 %copy-start.3 = (bf16[512,2048]{1,0:T(8,128)(2,1)S(1)}, bf16[512,2048]{1,0:T(8,128)(2,1)}, u32[]{:S(2)}) copy-start(bf16[512,2048]{1,0:T(8,128)(2,1)} %get-tuple-element.16) | copy-start | bytes 6291460
Sparse Core Ops, SparseCore 0:
  173.1 31.6 reduce-scatter.1

commit v3 on v2

--- a/solution.py
+++ b/solution.py
@@ -141,6 +141,93 @@
         array.reshape((-1,) + array.shape[2:]) if axis == 0 else array
         for array, axis in zip(gathered, axes)
     ]
+
+
+def project_kernel(
+    attended, weight, residual, out, sent_far, sent_near, sent_across, got_far, got_near, got_across,
+    send_sems, recv_sems,
+):
+    me = lax.axis_index("tp")
+    near = me + 1 - 2 * lax.rem(me, 2)
+    across = lax.rem(me + 2, 4)
+    far = lax.rem(near + 2, 4)
+    width = out.shape[1]
+    chunks = sent_far.shape[0]
+    rows = sent_far.shape[1]
+
+    def product(chunk, target):
+        columns = pl.ds(pl.multiple_of(target * width, width), width)
+        return jnp.dot(
+            attended[pl.ds(chunk * rows, rows), :],
+            weight[:, columns],
+            preferred_element_type=jnp.float32,
+        )
+
+    def copy(kind, sent, got, chunk, target):
+        return pltpu.make_async_remote_copy(
+            src_ref=sent.at[chunk],
+            dst_ref=got.at[chunk],
+            send_sem=send_sems.at[kind, chunk],
+            recv_sem=recv_sems.at[kind, chunk],
+            device_id={"tp": target},
+            device_id_type=pl.DeviceIdType.MESH,
+        )
+
+    def far_copy(chunk):
+        return copy(0, sent_far, got_far, chunk, near)
+
+    def near_copy(chunk):
+        return copy(1, sent_near, got_near, chunk, near)
+
+    def across_copy(chunk):
+        return copy(2, sent_across, got_across, chunk, across)
+
+    barrier = pltpu.get_barrier_semaphore()
+    for target in (near, across):
+        pl.semaphore_signal(
+            barrier, inc=1, device_id={"tp": target}, device_id_type=pl.DeviceIdType.MESH
+        )
+    pl.semaphore_wait(barrier, 2)
+    for chunk in range(chunks):
+        sent_far[chunk] = product(chunk, far).astype(sent_far.dtype)
+        far_copy(chunk).start()
+    for chunk in range(chunks):
+        mine = product(chunk, across)
+        far_copy(chunk).wait_recv()
+        sent_across[chunk] = (mine + got_far[chunk].astype(jnp.float32)).astype(sent_across.dtype)
+        across_copy(chunk).start()
+    for chunk in range(chunks):
+        sent_near[chunk] = product(chunk, near).astype(sent_near.dtype)
+        near_copy(chunk).start()
+    for chunk in range(chunks):
+        span = pl.ds(chunk * rows, rows)
+        total = product(chunk, me) + residual[span, :].astype(jnp.float32)
+        near_copy(chunk).wait_recv()
+        total = total + got_near[chunk].astype(jnp.float32)
+        across_copy(chunk).wait_recv()
+        out[span, :] = (total + got_across[chunk].astype(jnp.float32)).astype(out.dtype)
+    for chunk in range(chunks):
+        far_copy(chunk).wait_send()
+        across_copy(chunk).wait_send()
+        near_copy(chunk).wait_send()
+
+
+def project_and_scatter(attended, weight, residual):
+    row_total = attended.shape[0]
+    width = residual.shape[1]
+    chunks = 4
+    piece = pltpu.VMEM((chunks, row_total // chunks, width), jnp.bfloat16)
+    return pl.pallas_call(
+        project_kernel,
+        out_shape=jax.ShapeDtypeStruct(residual.shape, residual.dtype),
+        in_specs=[pl.BlockSpec(memory_space=pltpu.VMEM)] * 3,
+        out_specs=pl.BlockSpec(memory_space=pltpu.VMEM),
+        scratch_shapes=[piece] * 6
+        + [pltpu.SemaphoreType.DMA((3, chunks)), pltpu.SemaphoreType.DMA((3, chunks))],
+        compiler_params=pltpu.CompilerParams(
+            collective_id=1, has_side_effects=True, vmem_limit_bytes=32 * 1024 * 1024
+        ),
+    )(attended, weight, residual)
 
 
 def active_rows(stored, active_slots):
@@ -322,18 +409,16 @@
     attended = attend(query_per_head, key_heads, value_per_head, segment).reshape(
         row_total, local_width
     )
-    partial_out = jnp.dot(
-        attended,
-        output_full,
-        preferred_element_type=jnp.float32,
-    )
+    share_width = model_width // tp_total
+    residual_part = lax.dynamic_slice_in_dim(
+        tokens, lax.axis_index("tp") * share_width, share_width, 1
+    )
+    if tp_total == 4:
+        return project_and_scatter(attended, output_full, residual_part)
+    partial_out = jnp.dot(attended, output_full, preferred_element_type=jnp.float32)
     summed = lax.psum_scatter(
         partial_out.astype(jnp.bfloat16), "tp", scatter_dimension=1, tiled=True
     ).astype(jnp.float32)
-    share_width = summed.shape[1]
-    residual_part = lax.dynamic_slice_in_dim(
-        tokens, lax.axis_index("tp") * share_width, share_width, 1
-    )
     return (summed + residual_part.astype(jnp.float32)).astype(jnp.bfloat16)
 
 

time: 214 us -> 173 us (0.81)
  waiting for transfers between devices: 31.8 us -> 0 us
  Pallas kernels: 108 us -> 124 us
  between operations: 13.5 us -> 0.21 us
  other arithmetic: 14.2 us -> 5.07 us
  matrix products: 32.2 us -> 28 us
    reduce_scatter x1 -> x0, waiting for transfers between devices: 31.8 us -> none  [local(): lax.psum_scatter(partial_out.astype(jnp.bfloat16), 'tp', scatter_dimensio...]
    pallas_call x0 -> x1, Pallas kernels: none -> 16.2 us  [project_and_scatter(): pl.pallas_call(project_kernel, out_shape=jax.ShapeDtypeStruct(residual.sh...]
    dot_general x1 -> x0, matrix products: 2.64 us -> none  [local(): jnp.dot(attended, output_full, preferred_element_type=jnp.float32)]
    another operation x3, other arithmetic: 2.92 us -> 0.67 us
  transfers between devices with their start and end apart: 1 -> 0, of which waited for: 1 -> 0; matrix products, arithmetic and copies ran while one was open for 0% -> 0% of each run, Pallas kernels for 0% -> 0%
where the time goes in v3:
time: 173 us
  Pallas kernels  124 us (72%)
  matrix products  28 us (16%)
  local copies, waits for them, and re-layouts  10.1 us (6%)
  blocking collectives  5.39 us (3%)
  other arithmetic  5.07 us (3%)
    pallas_call x1, Pallas kernels, relay_gather(): pl.pallas_call(functools.partial(relay_kernel, lines, tuple(axes)), out_s...  108 us
    pallas_call x1, Pallas kernels, project_and_scatter(): pl.pallas_call(project_kernel, out_shape=jax.ShapeDtypeStruct(residual.sh...  16.2 us
    sub x1, matrix products, attend(): scores - row_peak  6.79 us
    all_gather x1, blocking collectives, local(): shrunk = lax.all_gather(shrunk_part, 'tp', axis=1, tiled=True)  5.39 us
    dot_general x1, matrix products, attend(): jnp.einsum('hqk,khd->qhd', weights, value_per_head, preferred_element_typ...  4.38 us
    dot_general x2, matrix products, change_of(): jnp.dot(spread, up_all[:, kind].reshape(place_total * reduced_rows, local...  4.18 us
    dot_general x1, local copies, waits for them, and re-layouts, local(): key_base = jnp.dot(normed, key_full, preferred_element_type=jnp.float32)  3.98 us
    dot_general x1, matrix products, local(): jnp.dot(normed, query_full, preferred_element_type=jnp.float32)  3.95 us

profile of v3, /device:TPU:0, one launch (start us, length us, event | category | flops | bytes accessed | tf_op | source)
XLA Modules:
  0.0 172.6 jit_solution(2303622427517151542)
XLA Ops:
  0.0 0.0 copy-start
  0.0 0.9 copy-done
  1.0 0.7 reshape_reshape.9.refs_0_
  1.6 107.7 %shard_map.118 = (bf16[8,16,2048]{2,1,0:T(8,128)(2,1)}, bf16[8,64,512]{2,1,0:T(8,128)(2,1)}, bf16[8,256,512]{2,1,0:T(8,128)(2,1)}, bf16[8,256,512]{2,1,0:T(8,128...) custom-call(bf16[16,2048]{1,0:T(8,128)(2,1)} %reshape_reshape.9.refs_0_, bf16[64,512]{1,0:T(8,128)(2,1)} %bitcast.49, ...), custom_call_target="tpu_custom_call" | custom-call | tf_op jit(solution)/shard_map/pallas_call | solution.py:118
  109.4 0.7 convert_element_type.47
  110.1 2.1 %fusion.2 = f32[512]{0:T(512)S(1)} fusion(bf16[512,2048]{1,0:T(8,128)(2,1)} %param.12), kind=kLoop, calls=%fused_computation.9 | loop fusion | flops 3145216 | bytes 2099200 | tf_op jit(solution)/shard_map/reduce_sum | solution.py:333
  112.1 0.0 copy-start.5
  112.2 0.0 copy-start.7
  112.2 0.0 copy-start.2
  112.2 0.0 copy-start.8
  112.2 0.0 copy-start.6
  112.2 0.0 copy-start.3
  112.2 3.8 %fusion.69 = f32[512,512]{0,1:T(8,128)S(1)} fusion(bf16[2048,512]{1,0:T(8,128)(2,1)} %bitcast.53, bf16[512,2048]{1,0:T(8,128)(2,1)} %param.12, f32[2048]{0:T(1024)S(1)} %convert_element_type.47, f32[512]{0:T(512)S(1)} %add_rsqrt_fusion), kind=kOutput, calls=%fused_computation.119 | convolution fusion | flops 1077936128 | bytes 5253120 | tf_op jit(solution)/shard_map/dot_general | solution.py:346
  116.0 0.0 copy-done.5
  116.0 0.8 fusion.71
  116.8 0.0 copy-done.7
  116.8 0.0 copy-done.2
  116.9 0.7 gather_fusion
  117.5 0.0 copy-done.8
  117.6 0.6 gather_fusion.1
  118.2 0.0 copy-done.6
  118.2 0.1 select_reduce_fusion
  118.3 0.0 copy-done.3
  118.3 2.0 %fusion.19 = bf16[512,8]{0,1:T(8,128)(2,1)S(1)} fusion(bf16[128,2048]{1,0:T(8,128)(2,1)} %bitcast.54, s32[128]{0:T(128)S(1)} %get-tuple-element.30, s32[512]{0:T(512)S(1)} %select_reduce_fusion, s32[128]{0:T(128)S(1)} %get-tuple-element.29, bf16[512,2048]{1,0:T(8,128)(2,1)S(1)} %copy-done.3, f32[2048]{0:T(1024)S(1)} %convert_element_type.47, ...), kind=kOutput, calls=%fused_computation.31 | convolution fusion | flops 273880064 | bytes 2642944 | tf_op jit(solution)/shard_map/dot_general | solution.py:368
  120.3 5.4 %all_gather.3 = bf16[512,32]{0,1:T(8,128)(2,1)S(1)} all-gather(bf16[512,8]{0,1:T(8,128)(2,1)S(1)} %fusion.19), channel_id=1, replica_groups=mesh['req'=8,'tp'=4] {'tp'}, dimensions={1}, use_global_device_ids=true | all-gather | bytes 40960 | tf_op jit(solution)/shard_map/all_gather | solution.py:371
  125.7 2.3 %fusion.14 = bf16[512,512]{0,1:T(8,128)(2,1)} fusion(f32[512,512]{0,1:T(8,128)S(1)} %fusion.69, bf16[256,512]{1,0:T(8,128)(2,1)} %bitcast.45, bf16[512,32]{0,1:T(8,128)(2,1)S(1)} %all_gather.3, s32[256]{0:T(256)S(1)} %get-tuple-element.34, s32[512]{0:T(512)S(1)} %select_reduce_fusion, s32[256]{0:T(256)S(1)} %get-tuple-element.33, s32[32]{0:T(128)S(1)} %fusion.52, ...), kind=kOutput, calls=%fused_computation.23 | convolution fusion | flops 143802368 | bytes 1872032 | tf_op jit(solution)/shard_map/dot_general | solution.py:387
  128.0 0.9 fusion.20
  128.9 3.9 %fusion.65 = f32[512,512]{0,1:T(8,128)} fusion(bf16[2048,512]{1,0:T(8,128)(2,1)} %bitcast.52, bf16[512,2048]{1,0:T(8,128)(2,1)S(1)} %copy-done.3, f32[2048]{0:T(1024)S(1)} %convert_element_type.47, f32[512]{0:T(512)S(1)} %add_rsqrt_fusion), kind=kOutput, calls=%fused_computation.118 | convolution fusion | flops 1077936128 | bytes 5253120 | tf_op jit(solution)/shard_map/dot_general | solution.py:336
  132.9 1.9 %fusion.11 = f32[512,512]{0,1:T(8,128)S(1)} fusion(f32[512,512]{0,1:T(8,128)} %fusion.65, bf16[256,512]{1,0:T(8,128)(2,1)} %bitcast.44, bf16[512,32]{0,1:T(8,128)(2,1)S(1)} %all_gather.3, s32[256]{0:T(256)S(1)} %get-tuple-element.34, s32[512]{0:T(512)S(1)} %select_reduce_fusion, s32[256]{0:T(256)S(1)} %get-tuple-element.33, s32[32]{0:T(128)S(1)} %fusion.52, ...), kind=kOutput, calls=%fused_computation.19 | convolution fusion | flops 143540224 | bytes 2396320 | tf_op jit(solution)/shard_map/dot_general | solution.py:387
  134.7 0.1 compare_reduce_fusion
  134.8 0.1 add_select_fusion
  134.9 0.3 reduce-window.9
  135.2 0.1 slice.38
  135.3 0.1 slice_reduce_fusion
  135.5 0.1 fusion.49
  135.5 0.3 multiply_cosine_fusion
  135.9 4.0 %copy.19 = bf16[512,2048]{1,0:T(8,128)(2,1)} copy(bf16[512,2048]{0,1:T(8,128)(2,1)} %bitcast.42) | data formatting | bytes 4194304 | tf_op jit(solution)/shard_map/dot_general | solution.py:341
  139.8 2.9 %fusion.9 = f32[512,8,64]{0,2,1:T(8,128)S(1)} fusion(bf16[8,64,2048]{2,1,0:T(8,128)(2,1)} %bitcast.43, bf16[512,2048]{1,0:T(8,128)(2,1)S(1)} %copy-done.3, f32[2048]{0:T(1024)S(1)} %convert_element_type.47, f32[512]{0:T(512)S(1)} %add_rsqrt_fusion), kind=kOutput, calls=%fused_computation.16 | convolution fusion | flops 1077936128 | bytes 5253120 | tf_op jit(solution)/shard_map/dot_general | solution.py:341
  142.8 0.3 subtract_convert_fusion.1
  143.1 0.0 copy-start.4
  143.1 6.8 %fusion.72 = (f32[8,512]{1,0:T(8,128)S(1)}, f32[8,512,512]{1,2,0:T(8,128)}) fusion(pred[512,512]{0,1:T(8,128)(4,1)} %fusion.20, bf16[512,8,32]{0,2,1:T(8,128)(2,1)S(1)} %get-tuple-element.23, bf16[512,8,32]{0,2,1:T(8,128)(2,1)S(1)} %get-tuple-element.24, bf16[512,8,32]{0,2,1:T(8,128)(2,1)S(1)} %get-tuple-element.18, ...), kind=kOutput, calls=%fused_computation.121 | convolution fusion | flops 281018880 | bytes 9715712 | tf_op jit(solution)/shard_map/sub | solution.py:277
  149.9 0.0 copy-done.4
  149.9 4.4 %fusion.13 = bf16[8,64,512]{2,1,0:T(8,128)(2,1)S(1)} fusion(bf16[512,8,64]{0,2,1:T(8,128)(2,1)S(1)} %bitcast.46, f32[8,512,512]{1,2,0:T(8,128)} %get-tuple-element.28, f32[8,512]{1,0:T(8,128)S(1)} %get-tuple-element.27), kind=kOutput, calls=%fused_computation.22 | convolution fusion | flops 272891904 | bytes 9453568 | tf_op jit(solution)/shard_map/hqk,khd->qhd/dot_general | solution.py:279
  154.3 0.2 copy.21.attended
  154.5 1.1 constant_dynamic-slice_fusion.residual
  155.6 0.0 copy-done.1
  155.6 16.2 %shard_map.119 = bf16[512,512]{1,0:T(8,128)(2,1)S(1)} custom-call(bf16[512,512]{1,0:T(8,128)(2,1)S(1)} %copy.21.attended, bf16[512,2048]{1,0:T(8,128)(2,1)S(1)} %copy-done.1, bf16[512,512]{1,0:T(8,128)(2,1)S(1)} %constant_dynamic-slice_fusion.residual), custom_call_target="tpu_custom_call" | custom-call | tf_op jit(solution)/shard_map/pallas_call | solution.py:220
  171.8 0.8 copy.24
  (14 shorter events, 0.1 us)
Async XLA Ops:
  0.0 1.0 copy-start
  112.1 3.8 %copy-start.5 = (bf16[8,64,512]{2,1,0:T(8,128)(2,1)S(1)}, bf16[8,64,512]{2,1,0:T(8,128)(2,1)}, u32[]{:S(2)}) copy-start(bf16[8,64,512]{2,1,0:T(8,128)(2,1)} %get-tuple-element.13) | copy-start | bytes 1572868
  112.2 4.7 %copy-start.7 = (s32[16]{0:T(128)S(1)}, s32[16]{0:T(128)}, u32[]{:S(2)}) copy-start(s32[16]{0:T(128)} %param.15) | copy-start | bytes 196
  112.2 4.7 %copy-start.2 = (s32[16]{0:T(128)S(1)}, s32[16]{0:T(128)}, u32[]{:S(2)}) copy-start(s32[16]{0:T(128)} %param.16) | copy-start | bytes 196
  112.2 5.4 %copy-start.8 = (s32[1,8]{1,0:T(1,128)S(1)}, s32[1,8]{1,0:T(1,128)}, u32[]{:S(2)}) copy-start(s32[1,8]{1,0:T(1,128)} %param.14) | copy-start | bytes 100
  112.2 6.0 %copy-start.6 = (s32[1,512]{1,0:T(1,128)S(1)}, s32[1,512]{1,0:T(1,128)}, u32[]{:S(2)}) copy-start(s32[1,512]{1,0:T(1,128)} %param.13) | copy-start | bytes 6148
  112.2 6.1 %copy-start.3 = (bf16[512,2048]{1,0:T(8,128)(2,1)S(1)}, bf16[512,2048]{1,0:T(8,128)(2,1)}, u32[]{:S(2)}) copy-start(bf16[512,2048]{1,0:T(8,128)(2,1)} %param.12) | copy-start | bytes 6291460
  143.1 6.8 %copy-start.4 = (bf16[512,512]{0,1:T(8,128)(2,1)S(1)}, bf16[512,512]{0,1:T(8,128)(2,1)}, u32[]{:S(2)}) copy-start(bf16[512,512]{0,1:T(8,128)(2,1)} %fusion.14) | copy-start | bytes 1572868
  149.9 5.7 %copy-start.1 = (bf16[512,2048]{1,0:T(8,128)(2,1)S(1)}, bf16[512,2048]{1,0:T(8,128)(2,1)}, u32[]{:S(2)}) copy-start(bf16[512,2048]{1,0:T(8,128)(2,1)} %get-tuple-element.16.weight) | copy-start | bytes 6291460

commit v4 on v3

--- a/solution.py
+++ b/solution.py
@@ -15,14 +15,20 @@
 adapter_scale = 2.0
 
 
-def relay_kernel(lines, axes, *refs):
+def relay_kernel(lines, axes, early, tp_total, *refs):
     count = len(axes)
-    sources, gathered = refs[:count], refs[count : 2 * count]
-    send_sems, recv_sems, local_sems = refs[2 * count :]
+    sources = refs[:count]
+    normed, mask, fold = refs[count : count + 3]
+    up_all, output_all, query_out, key_out, value_out, shrunk_out = refs[count + 3 : count + 9]
+    down_all, query_all, key_all, value_all, shrunk_got = refs[count + 9 : count + 14]
+    send_sems, recv_sems, local_sems, shrunk_send, shrunk_recv = refs[count + 14 :]
+    gathered = (down_all, up_all, query_all, key_all, value_all, output_all)
     me = lax.axis_index("req")
+    part = lax.axis_index("tp")
     line = lax.div(me, 2)
     side = lax.rem(me, 2)
     partner = 2 * line + 1 - side
+    turn = 1 - 2 * side
     has_up = line < lines - 1
     has_down = line > 0
 
@@ -46,101 +52,180 @@
     def arrival(index, origin):
         to_device(index, origin, 3, partner).wait_recv()
 
+    def own_copies(index, act):
+        pl.when(has_up)(lambda: act(to_device(index, me, 0, me + 2)))
+        pl.when(has_down)(lambda: act(to_device(index, me, 1, me - 2)))
+        act(to_device(index, me, 2, partner))
+
+    def pair_copies(index, act):
+        pl.when(has_up)(lambda: act(to_device(index, partner, 3, me + 2)))
+        pl.when(has_down)(lambda: act(to_device(index, partner, 4, me - 2)))
+
+    def step_copies(index, step, act, receive):
+        slot = 5 + 4 * (step - 1)
+
+        for below, base, edge in ((True, slot, 2), (False, slot + 2, -2)):
+            if below:
+                origin = me - 2 * step
+                held = line >= step
+                onward = jnp.minimum(line - step, lines - 2 - line) >= 0
+            else:
+                origin = me + 2 * step
+                held = line + step < lines
+                onward = jnp.minimum(line - 1, lines - 1 - step - line) >= 0
+            if index in early:
+                if receive:
+
+                    @pl.when(held)
+                    def _():
+                        arrival(index, origin)
+                        arrival(index, origin + turn)
+
+                @pl.when(onward)
+                def _():
+                    act(to_device(index, origin, base, me + edge))
+                    act(to_device(index, origin + turn, base + 1, me + edge))
+
+            else:
+
+                @pl.when(held)
+                def _():
+                    if receive:
+                        arrival(index, origin)
+                    act(to_device(index, origin, base + 1, partner))
+
+                @pl.when(onward)
+                def _():
+                    act(to_device(index, origin, base, me + edge))
+
+    def start(copy):
+        copy.start()
+
+    def finish(copy):
+        copy.wait_send()
+
+    def local_copy(index):
+        return pltpu.make_async_copy(sources[index], block(index, me), local_sems.at[index])
+
+    def complete(index):
+        if index not in early:
+            for other in range(lines):
+                arrival(index, 2 * other + 1 - side)
+        local_copy(index).wait()
+
+    def shrunk_copy(hop):
+        return pltpu.make_async_remote_copy(
+            src_ref=shrunk_out,
+            dst_ref=shrunk_got.at[hop - 1],
+            send_sem=shrunk_send.at[hop - 1],
+            recv_sem=shrunk_recv.at[hop - 1],
+            device_id={"tp": lax.rem(part + hop, tp_total)},
+            device_id_type=pl.DeviceIdType.MESH,
+        )
+
     barrier = pltpu.get_barrier_semaphore()
 
-    def greet(target):
+    def greet(device):
         pl.semaphore_signal(
-            barrier, inc=1, device_id={"req": target}, device_id_type=pl.DeviceIdType.MESH
-        )
-
-    greet(partner)
-    pl.when(has_up)(lambda: greet(me + 2))
-    pl.when(has_down)(lambda: greet(me - 2))
-    pl.semaphore_wait(barrier, 1 + has_up.astype(jnp.int32) + has_down.astype(jnp.int32))
+            barrier, inc=1, device_id=device, device_id_type=pl.DeviceIdType.MESH
+        )
+
+    greet({"req": partner})
+    pl.when(has_up)(lambda: greet({"req": me + 2}))
+    pl.when(has_down)(lambda: greet({"req": me - 2}))
+    for hop in range(1, tp_total):
+        greet({"tp": lax.rem(part + hop, tp_total)})
+    pl.semaphore_wait(barrier, tp_total + has_up.astype(jnp.int32) + has_down.astype(jnp.int32))
 
     for index in range(count):
-        pl.when(has_up)(lambda: to_device(index, me, 0, me + 2).start())
-        pl.when(has_down)(lambda: to_device(index, me, 1, me - 2).start())
-        to_device(index, me, 2, partner).start()
+        own_copies(index, start)
     for index in range(count):
-        pltpu.make_async_copy(sources[index], block(index, me), local_sems.at[index]).start()
+        local_copy(index).start()
+    for index in early:
+        arrival(index, partner)
+        pair_copies(index, start)
     for step in range(1, lines):
-        slot = 3 + 4 * (step - 1)
         for index in range(count):
-
-            @pl.when(line >= step)
-            def _():
-                origin = me - 2 * step
-                arrival(index, origin)
-                pl.when(has_up)(lambda: to_device(index, origin, slot, me + 2).start())
-                to_device(index, origin, slot + 1, partner).start()
-
-            @pl.when(line + step < lines)
-            def _():
-                origin = me + 2 * step
-                arrival(index, origin)
-                pl.when(has_down)(lambda: to_device(index, origin, slot + 2, me - 2).start())
-                to_device(index, origin, slot + 3, partner).start()
-
+            step_copies(index, step, start, True)
+
+    rows = normed.shape[0] // 2
+
+    complete(0)
+    down = down_all[...].reshape(-1, down_all.shape[2])
+    shrunk = lax.dot_general(
+        normed[...], down, (((1,), (1,)), ((), ())), preferred_element_type=jnp.float32
+    ).astype(jnp.bfloat16)
+    shrunk_out[...] = jnp.dot(
+        shrunk * mask[...], fold[...], preferred_element_type=jnp.float32
+    ).astype(jnp.bfloat16)
+    for hop in range(1, tp_total):
+        shrunk_copy(hop).start()
+    complete(1)
+    for index, result in ((2, query_out), (3, key_out), (4, value_out)):
+        complete(index)
+
+        def one(piece, carry):
+            span = pl.ds(pl.multiple_of(piece * rows, rows), rows)
+            weight = gathered[index][...].reshape(-1, gathered[index].shape[2])
+            result[span, :] = jnp.dot(
+                normed[span, :], weight, preferred_element_type=jnp.float32
+            )
+            return carry
+
+        lax.fori_loop(0, 2, one, 0)
+    for hop in range(1, tp_total):
+        shrunk_copy(hop).wait()
+    total = shrunk_out[...]
+    for hop in range(1, tp_total):
+        total = total + shrunk_got[hop - 1]
+    shrunk_out[...] = total
+    complete(5)
     for index in range(count):
-        for other in range(lines):
-            arrival(index, 2 * other + 1 - side)
-        pltpu.make_async_copy(sources[index], block(index, me), local_sems.at[index]).wait()
-        pl.when(has_up)(lambda: to_device(index, me, 0, me + 2).wait_send())
-        pl.when(has_down)(lambda: to_device(index, me, 1, me - 2).wait_send())
-        to_device(index, me, 2, partner).wait_send()
+        own_copies(index, finish)
+        if index in early:
+            pair_copies(index, finish)
         for step in range(1, lines):
-            slot = 3 + 4 * (step - 1)
-
-            @pl.when(line >= step)
-            def _():
-                origin = me - 2 * step
-                pl.when(has_up)(lambda: to_device(index, origin, slot, me + 2).wait_send())
-                to_device(index, origin, slot + 1, partner).wait_send()
-
-            @pl.when(line + step < lines)
-            def _():
-                origin = me + 2 * step
-                pl.when(has_down)(lambda: to_device(index, origin, slot + 2, me - 2).wait_send())
-                to_device(index, origin, slot + 3, partner).wait_send()
-
-
-def relay_gather(arrays, axes, req_total):
+            step_copies(index, step, finish, False)
+
+
+def relay_project(arrays, normed, mask, fold, req_total, tp_total):
     lines = req_total // 2
+    axes = (0, 0, 0, 0, 0, 1)
     count = len(arrays)
-    shapes = []
-    for array, axis in zip(arrays, axes):
-        if axis == 0:
-            shape = (req_total,) + array.shape
-        else:
-            shape = (array.shape[0], req_total * array.shape[1])
-        shapes.append(jax.ShapeDtypeStruct(shape, array.dtype))
+    up, weight, output = arrays[1], arrays[2], arrays[5]
+    row_total = normed.shape[0]
+    base = jax.ShapeDtypeStruct((row_total, weight.shape[1]), jnp.float32)
+    whole = pltpu.VMEM((req_total,) + weight.shape, weight.dtype)
+    in_vmem = pl.BlockSpec(memory_space=pltpu.VMEM)
+    anywhere = pl.BlockSpec(memory_space=pl.ANY)
     return pl.pallas_call(
-        functools.partial(relay_kernel, lines, tuple(axes)),
-        out_shape=shapes,
-        in_specs=[pl.BlockSpec(memory_space=pl.ANY)] * count,
-        out_specs=[pl.BlockSpec(memory_space=pl.ANY)] * count,
+        functools.partial(relay_kernel, lines, axes, (0, 1), tp_total),
+        out_shape=[
+            jax.ShapeDtypeStruct((req_total,) + up.shape, up.dtype),
+            jax.ShapeDtypeStruct((output.shape[0], req_total * output.shape[1]), output.dtype),
+            base,
+            base,
+            base,
+            jax.ShapeDtypeStruct((row_total, fold.shape[1]), jnp.bfloat16),
+        ],
+        in_specs=[anywhere] * count + [in_vmem] * 3,
+        out_specs=[anywhere] * 2 + [in_vmem] * 4,
         scratch_shapes=[
-            pltpu.SemaphoreType.DMA((count, 3 + 4 * (lines - 1))),
+            pltpu.VMEM((req_total,) + arrays[0].shape, arrays[0].dtype),
+            whole,
+            whole,
+            whole,
+            pltpu.VMEM((tp_total - 1, row_total, fold.shape[1]), jnp.bfloat16),
+            pltpu.SemaphoreType.DMA((count, 5 + 4 * (lines - 1))),
             pltpu.SemaphoreType.DMA((count, req_total)),
             pltpu.SemaphoreType.DMA((count,)),
+            pltpu.SemaphoreType.DMA((tp_total - 1,)),
+            pltpu.SemaphoreType.DMA((tp_total - 1,)),
         ],
-        compiler_params=pltpu.CompilerParams(collective_id=0, has_side_effects=True),
-    )(*arrays)
-
-
-def gather_all(arrays, axes, req_total):
-    if req_total % 2 == 0 and req_total <= 16:
-        gathered = relay_gather(arrays, axes, req_total)
-    else:
-        gathered = [
-            lax.all_gather(array, "req", axis=axis, tiled=axis == 1)
-            for array, axis in zip(arrays, axes)
-        ]
-    return [
-        array.reshape((-1,) + array.shape[2:]) if axis == 0 else array
-        for array, axis in zip(gathered, axes)
-    ]
+        compiler_params=pltpu.CompilerParams(
+            collective_id=0, has_side_effects=True, vmem_limit_bytes=40 * 1024 * 1024
+        ),
+    )(*arrays, normed, mask, fold)
 
 
 def project_kernel(
@@ -310,65 +395,63 @@
     ).reshape(slot_total, share, model_width)
     up_part = adapter_up_weight.reshape(slot_total, 2 * reduced_rows, local_width)
     active_slots = jnp.take(adapter_storage_slot, adapters_in_use, axis=0)
-    arrays = [query_weight, key_weight, value_weight, output_weight]
-    axes = [0, 0, 0, 1]
-    if slot_total * req_total <= 2 * active_slots.shape[0]:
-        adapter_parts = [
-            down_part.reshape(slot_total * share, model_width),
-            up_part.reshape(slot_total * 2 * reduced_rows, local_width),
-        ]
-        down_all, up_all, query_full, key_full, value_full, output_full = gather_all(
-            adapter_parts + arrays, [0, 0] + axes, req_total
-        )
-        request_places = active_slots[request_adapters]
-    else:
-        down_all = active_rows(down_part, active_slots)
-        up_all = active_rows(up_part, active_slots)
-        query_full, key_full, value_full, output_full = gather_all(arrays, axes, req_total)
-        request_places = request_adapters
-    place_total = down_all.shape[0] // share
     floats = tokens.astype(jnp.float32)
     normed = (
         floats
         * lax.rsqrt(jnp.mean(floats * floats, axis=-1, keepdims=True) + norm_eps)
         * input_norm_gain.astype(jnp.float32)
     ).astype(jnp.bfloat16)
-    query_plain = jnp.dot(
-        normed,
-        query_full,
-        preferred_element_type=jnp.float32,
-    )
-    key_base = jnp.dot(
-        normed,
-        key_full,
-        preferred_element_type=jnp.float32,
-    )
-    value_plain = jnp.dot(
-        normed,
-        value_full,
-        preferred_element_type=jnp.float32,
-    )
-    request_total = request_adapters.shape[0]
-    member = segment[:, None] == jnp.arange(request_total, dtype=jnp.int32)[None, :]
+    relayed = req_total % 2 == 0 and req_total <= 16
+    relayed = relayed and slot_total * req_total <= 2 * active_slots.shape[0]
+    if relayed:
+        place_total = slot_total * req_total
+        request_places = active_slots[request_adapters]
+    else:
+        place_total = active_slots.shape[0]
+        request_places = request_adapters
+    member = segment[:, None] == jnp.arange(request_adapters.shape[0], dtype=jnp.int32)[None, :]
     token_place = jnp.sum(
         jnp.where(member, request_places[None, :], jnp.zeros_like(request_places)[None, :]),
         axis=1,
     )
-    shrunk_all = lax.dot_general(
-        normed,
-        down_all,
-        (((1,), (1,)), ((), ())),
-        preferred_element_type=jnp.float32,
-    ).astype(jnp.bfloat16)
     column = jnp.arange(place_total * share, dtype=jnp.int32)
-    kept = jnp.where(
-        token_place[:, None] == (column // share)[None, :], shrunk_all, jnp.zeros((), jnp.bfloat16)
-    )
-    fold = (column % share)[:, None] == jnp.arange(share, dtype=jnp.int32)[None, :]
-    shrunk_part = jnp.dot(
-        kept, fold.astype(jnp.bfloat16), preferred_element_type=jnp.float32
-    ).astype(jnp.bfloat16)
-    shrunk = lax.all_gather(shrunk_part, "tp", axis=1, tiled=True)
+    mask = (token_place[:, None] == (column // share)[None, :]).astype(jnp.bfloat16)
+    lanes = max(128, tp_total * share)
+    fold = (lax.axis_index("tp") * share + column % share)[:, None] == jnp.arange(
+        lanes, dtype=jnp.int32
+    )[None, :]
+    fold = fold.astype(jnp.bfloat16)
+    if relayed:
+        arrays = [
+            down_part.reshape(slot_total * share, model_width),
+            up_part.reshape(slot_total * 2 * reduced_rows, local_width),
+            query_weight,
+            key_weight,
+            value_weight,
+            output_weight,
+        ]
+        up_all, output_full, query_plain, key_base, value_plain, shrunk = relay_project(
+            arrays, normed, mask, fold, req_total, tp_total
+        )
+    else:
+        down_all = active_rows(down_part, active_slots)
+        up_all = active_rows(up_part, active_slots)
+        output_full = lax.all_gather(output_weight, "req", axis=1, tiled=True)
+        query_plain, key_base, value_plain = [
+            jnp.dot(
+                normed,
+                lax.all_gather(weight, "req", axis=0, tiled=True),
+                preferred_element_type=jnp.float32,
+            )
+            for weight in (query_weight, key_weight, value_weight)
+        ]
+        shrunk_all = lax.dot_general(
+            normed, down_all, (((1,), (1,)), ((), ())), preferred_element_type=jnp.float32
+        ).astype(jnp.bfloat16)
+        shrunk = lax.psum(
+            jnp.dot(shrunk_all * mask, fold, preferred_element_type=jnp.float32), "tp"
+        ).astype(jnp.bfloat16)
+    shrunk = shrunk[:, : tp_total * share]
     source = jnp.arange(tp_total * share, dtype=jnp.int32)
     source_kind = (source % share) // part_rows
     source_rank = (source // share) * part_rows + source % part_rows

time: 173 us -> 163 us (0.942)
  matrix products: 28 us -> 14.9 us
  local copies, waits for them, and re-layouts: 10.1 us -> 17.6 us
  blocking collectives: 5.39 us -> 0 us
  other arithmetic: 5.07 us -> 8.58 us
  Pallas kernels: 124 us -> 121 us
    dot_general x4 -> x0, matrix products: 12.6 us -> none  [the longest x1 3.95 us: local(): jnp.dot(normed, query_full, preferred_element_type=jnp.float32)]
    unnamed x19 -> x37, local copies, waits for them, and re-layouts: 1.79 us -> 10.6 us
    all_gather x1 -> x0, blocking collectives: 5.39 us -> none  [local(): shrunk = lax.all_gather(shrunk_part, 'tp', axis=1, tiled=True)]
    dot_general x1 -> x0, local copies, waits for them, and re-layouts: 3.98 us -> none  [local(): key_base = jnp.dot(normed, key_full, preferred_element_type=jnp.float32)]
    pallas_call x1, Pallas kernels: 108 us -> 104 us  [relay_project(): pl.pallas_call(functools.partial(relay_kernel, lines, axes, (0, 1), tp_to...]
    convert_element_type x0 -> x3, other arithmetic: none -> 2.36 us  [the longest x1 2.14 us: local(): normed = (floats * lax.rsqrt(jnp.mean(floats * floats, axis=-1, keepdims=...]
    convert_element_type x0 -> x1, local copies, waits for them, and re-layouts: none -> 2.07 us  [local(): value_per_head = (value_plain + adapter_scale * value_change).astype(jnp....]
where the time goes in v4:
time: 163 us; the launch traced here: 162 us
  Pallas kernels  121 us (74%)
  local copies, waits for them, and re-layouts  17.6 us (11%)
  matrix products  14.9 us (9%)
  other arithmetic  8.58 us (5%)
    pallas_call x1, Pallas kernels, relay_project(): pl.pallas_call(functools.partial(relay_kernel, lines, axes, (0, 1), tp_to...  104 us
    pallas_call x1, Pallas kernels, project_and_scatter(): pl.pallas_call(project_kernel, out_shape=jax.ShapeDtypeStruct(residual.sh...  16.2 us
    unnamed x37, local copies, waits for them, and re-layouts  10.6 us
    sub x1, matrix products, attend(): scores - row_peak  6.8 us
    dot_general x1, matrix products, attend(): jnp.einsum('hqk,khd->qhd', weights, value_per_head, preferred_element_typ...  4.38 us
    dot_general x2, matrix products, change_of(): jnp.dot(spread, up_all[:, kind].reshape(place_total * reduced_rows, local...  3.68 us

profile of v4, /device:TPU:0, one launch (start us, length us, event | category | flops | bytes accessed | tf_op | source)
XLA Modules:
  0.0 162.0 jit_solution(5221465668584706032)
XLA Ops:
  0.0 0.0 copy-start
  0.0 0.0 copy-start.15
  0.0 0.9 copy-done
  1.0 0.7 reshape_reshape.6.refs_0_
  1.7 0.7 convert_element_type.46
  2.3 2.1 %fusion.2 = f32[512]{0:T(512)S(1)} fusion(bf16[512,2048]{1,0:T(8,128)(2,1)} %param.12), kind=kLoop, calls=%fused_computation.9 | loop fusion | flops 3145216 | bytes 2099200 | tf_op jit(solution)/shard_map/reduce_sum | solution.py:401
  4.4 2.1 %fusion.4.refs_6_ = bf16[512,2048]{1,0:T(8,128)(2,1)S(1)} fusion(bf16[512,2048]{1,0:T(8,128)(2,1)} %param.12, f32[2048]{0:T(1024)S(1)} %convert_element_type.46, f32[512]{0:T(512)S(1)} %add_rsqrt_fusion), kind=kLoop, calls=%fused_computation.11 | loop fusion | flops 4194304 | bytes 4204544 | tf_op jit(solution)/shard_map/convert_element_type | solution.py:403
  6.6 0.7 gather_fusion
  7.3 0.6 gather_fusion.1
  8.0 0.0 copy-done.15
  8.0 0.1 select_reduce_fusion
  8.1 0.1 compare_convert_fusion.refs_7_
  8.2 0.1 fusion.31.refs_8_
  8.3 0.0 copy-start.7
  8.3 0.9 copy-done.7
  9.3 0.9 copy-done.8
  10.2 0.9 copy-done.9
  11.2 0.9 copy-done.10
  12.1 0.8 copy-done.11
  13.0 0.8 copy-done.12
  13.8 104.4 %shard_map.118 = (bf16[8,64,512]{2,1,0:T(8,128)(2,1)S(1)}, bf16[512,2048]{1,0:T(8,128)(2,1)S(1)}, f32[512,512]{1,0:T(8,128)S(1)}, f32[512,512]{1,0:T(8,128)S(1)}...) custom-call(bf16[16,2048]{1,0:T(8,128)(2,1)S(1)} %copy-done.11, bf16[64,512]{1,0:T(8,128)(2,1)S(1)} %bitcast.27, ...), custom_call_target="tpu_custom_call" | custom-call | tf_op jit(solution)/shard_map/pallas_call | solution.py:201
  118.3 1.4 copy-done.1
  119.6 1.0 copy-done.3
  120.6 1.0 copy-done.5
  121.6 0.8 fusion.59
  122.4 0.6 fusion.48
  123.0 0.6 broadcast_compare_fusion
  123.6 2.2 %fusion.12 = bf16[512,512]{1,0:T(8,128)(2,1)} fusion(f32[512,512]{1,0:T(8,128)S(1)} %get-tuple-element.11, bf16[256,512]{1,0:T(8,128)(2,1)} %bitcast.31, s32[256]{0:T(256)S(1)} %get-tuple-element.34, s32[512]{0:T(512)S(1)} %select_reduce_fusion, bf16[512,128]{1,0:T(8,128)(2,1)S(1)} %get-tuple-element.12, s32[256]{0:T(256)S(1)} %get-tuple-element.33, ...), kind=kOutput, calls=%fused_computation.21 | convolution fusion | flops 143802368 | bytes 1970336 | tf_op jit(solution)/shard_map/dot_general | solution.py:470
  125.9 2.1 %copy.30 = bf16[512,512]{0,1:T(8,128)(2,1)} copy(bf16[512,512]{1,0:T(8,128)(2,1)} %fusion.12) | data formatting | bytes 1048576 | tf_op jit(solution)/shard_map/convert_element_type | solution.py:489
  127.9 0.9 fusion.15
  128.8 1.4 fusion.9
  130.3 0.3 copy.32
  130.6 0.1 compare_reduce_fusion
  130.7 0.1 add_select_fusion
  130.8 0.3 reduce-window.9
  131.1 0.1 slice.42
  131.2 0.1 slice_reduce_fusion
  131.4 0.1 fusion.44
  131.4 0.3 multiply_cosine_fusion
  131.8 0.3 copy.33
  132.1 0.3 subtract_convert_fusion.1
  132.4 6.8 %fusion.60 = (f32[8,512]{1,0:T(8,128)S(1)}, f32[8,512,512]{1,2,0:T(8,128)}) fusion(pred[512,512]{0,1:T(8,128)(4,1)} %fusion.15, bf16[512,8,32]{0,2,1:T(8,128)(2,1)S(1)} %get-tuple-element.23, bf16[512,8,32]{0,2,1:T(8,128)(2,1)S(1)} %get-tuple-element.24, bf16[512,8,32]{0,2,1:T(8,128)(2,1)S(1)} %get-tuple-element.18, ...), kind=kOutput, calls=%fused_computation.112 | convolution fusion | flops 281018880 | bytes 9715712 | tf_op jit(solution)/shard_map/sub | solution.py:362
  139.2 0.0 copy-done.14
  139.2 4.4 %fusion.11 = bf16[8,64,512]{2,1,0:T(8,128)(2,1)S(1)} fusion(bf16[512,8,64]{0,2,1:T(8,128)(2,1)S(1)} %bitcast.32, f32[8,512,512]{1,2,0:T(8,128)} %get-tuple-element.28, f32[8,512]{1,0:T(8,128)S(1)} %get-tuple-element.27), kind=kOutput, calls=%fused_computation.20 | convolution fusion | flops 272891904 | bytes 9453568 | tf_op jit(solution)/shard_map/hqk,khd->qhd/dot_general | solution.py:364
  143.6 0.2 copy.35.attended
  143.9 1.1 constant_dynamic-slice_fusion.residual
  144.9 16.2 %shard_map.119 = bf16[512,512]{1,0:T(8,128)(2,1)S(1)} custom-call(bf16[512,512]{1,0:T(8,128)(2,1)S(1)} %copy.35.attended, bf16[512,2048]{1,0:T(8,128)(2,1)S(1)} %copy-done.2, bf16[512,512]{1,0:T(8,128)(2,1)S(1)} %constant_dynamic-slice_fusion.residual), custom_call_target="tpu_custom_call" | custom-call | tf_op jit(solution)/shard_map/pallas_call | solution.py:305
  161.2 0.8 copy.40
  (32 shorter events, 0.2 us)
Async XLA Ops:
  0.0 1.0 copy-start
  0.0 6.6 %copy-start.13 = (s32[16]{0:T(128)S(1)}, s32[16]{0:T(128)}, u32[]{:S(2)}) copy-start(s32[16]{0:T(128)} %param.16) | copy-start | bytes 196
  0.0 6.6 %copy-start.16 = (s32[16]{0:T(128)S(1)}, s32[16]{0:T(128)}, u32[]{:S(2)}) copy-start(s32[16]{0:T(128)} %param.15) | copy-start | bytes 196
  0.0 7.3 %copy-start.17 = (s32[1,8]{1,0:T(1,128)S(1)}, s32[1,8]{1,0:T(1,128)}, u32[]{:S(2)}) copy-start(s32[1,8]{1,0:T(1,128)} %param.14) | copy-start | bytes 100
  0.0 8.0 %copy-start.15 = (s32[1,512]{1,0:T(1,128)S(1)}, s32[1,512]{1,0:T(1,128)}, u32[]{:S(2)}) copy-start(s32[1,512]{1,0:T(1,128)} %param.13) | copy-start | bytes 6148
  8.3 1.0 copy-start.7
  9.3 0.9 copy-start.8
  10.2 0.9 copy-start.9
  11.2 0.9 copy-start.10
  12.1 0.8 copy-start.11
  13.0 0.8 copy-start.12
  118.2 1.4 copy-start.1
  119.6 1.0 copy-start.3
  120.6 1.0 copy-start.5
  121.6 7.2 %copy-start.6 = (f32[512,512]{1,0:T(8,128)S(1)}, f32[512,512]{1,0:T(8,128)}, u32[]{:S(2)}) copy-start(f32[512,512]{1,0:T(8,128)} %copy-done.5) | copy-start | bytes 3145732
  122.4 9.3 %copy-start.4 = (f32[512,512]{1,0:T(8,128)S(1)}, f32[512,512]{1,0:T(8,128)}, u32[]{:S(2)}) copy-start(f32[512,512]{1,0:T(8,128)} %copy-done.3) | copy-start | bytes 3145732
  132.4 6.8 %copy-start.14 = (bf16[512,512]{0,1:T(8,128)(2,1)S(1)}, bf16[512,512]{0,1:T(8,128)(2,1)}, u32[]{:S(2)}) copy-start(bf16[512,512]{0,1:T(8,128)(2,1)} %copy.30) | copy-start | bytes 1572868
  139.2 5.7 %copy-start.2 = (bf16[512,2048]{1,0:T(8,128)(2,1)S(1)}, bf16[512,2048]{1,0:T(8,128)(2,1)}, u32[]{:S(2)}) copy-start(bf16[512,2048]{1,0:T(8,128)(2,1)} %copy-done.1) | copy-start | bytes 6291460

commit v5 on v4

--- a/solution.py
+++ b/solution.py
@@ -18,10 +18,10 @@
 def relay_kernel(lines, axes, early, tp_total, *refs):
     count = len(axes)
     sources = refs[:count]
-    normed, mask, fold = refs[count : count + 3]
-    up_all, output_all, query_out, key_out, value_out, shrunk_out = refs[count + 3 : count + 9]
-    down_all, query_all, key_all, value_all, shrunk_got = refs[count + 9 : count + 14]
-    send_sems, recv_sems, local_sems, shrunk_send, shrunk_recv = refs[count + 14 :]
+    tokens, gain, mask, fold = refs[count : count + 4]
+    up_all, output_all, query_out, key_out, value_out, shrunk_out = refs[count + 4 : count + 10]
+    down_all, query_all, key_all, value_all, shrunk_got, normed = refs[count + 10 : count + 16]
+    send_sems, recv_sems, local_sems, shrunk_send, shrunk_recv = refs[count + 16 :]
     gathered = (down_all, up_all, query_all, key_all, value_all, output_all)
     me = lax.axis_index("req")
     part = lax.axis_index("tp")
@@ -141,6 +141,18 @@
         own_copies(index, start)
     for index in range(count):
         local_copy(index).start()
+    norm_rows = normed.shape[0] // 8
+
+    def normalise(piece, carry):
+        span = pl.ds(pl.multiple_of(piece * norm_rows, norm_rows), norm_rows)
+        floats = tokens[span, :].astype(jnp.float32)
+        mean = jnp.mean(floats * floats, axis=-1, keepdims=True)
+        normed[span, :] = (
+            floats * lax.rsqrt(mean + norm_eps) * gain[...].astype(jnp.float32)
+        ).astype(normed.dtype)
+        return carry
+
+    lax.fori_loop(0, 8, normalise, 0)
     for index in early:
         arrival(index, partner)
         pair_copies(index, start)
@@ -188,12 +200,12 @@
             step_copies(index, step, finish, False)
 
 
-def relay_project(arrays, normed, mask, fold, req_total, tp_total):
+def relay_project(arrays, tokens, gain, mask, fold, req_total, tp_total):
     lines = req_total // 2
     axes = (0, 0, 0, 0, 0, 1)
     count = len(arrays)
     up, weight, output = arrays[1], arrays[2], arrays[5]
-    row_total = normed.shape[0]
+    row_total = tokens.shape[0]
     base = jax.ShapeDtypeStruct((row_total, weight.shape[1]), jnp.float32)
     whole = pltpu.VMEM((req_total,) + weight.shape, weight.dtype)
     in_vmem = pl.BlockSpec(memory_space=pltpu.VMEM)
@@ -208,7 +220,7 @@
             base,
             jax.ShapeDtypeStruct((row_total, fold.shape[1]), jnp.bfloat16),
         ],
-        in_specs=[anywhere] * count + [in_vmem] * 3,
+        in_specs=[pl.BlockSpec(memory_space=pltpu.HBM)] * count + [in_vmem] * 4,
         out_specs=[anywhere] * 2 + [in_vmem] * 4,
         scratch_shapes=[
             pltpu.VMEM((req_total,) + arrays[0].shape, arrays[0].dtype),
@@ -216,6 +228,7 @@
             whole,
             whole,
             pltpu.VMEM((tp_total - 1, row_total, fold.shape[1]), jnp.bfloat16),
+            pltpu.VMEM(tokens.shape, jnp.bfloat16),
             pltpu.SemaphoreType.DMA((count, 5 + 4 * (lines - 1))),
             pltpu.SemaphoreType.DMA((count, req_total)),
             pltpu.SemaphoreType.DMA((count,)),
@@ -225,7 +238,7 @@
         compiler_params=pltpu.CompilerParams(
             collective_id=0, has_side_effects=True, vmem_limit_bytes=40 * 1024 * 1024
         ),
-    )(*arrays, normed, mask, fold)
+    )(*arrays, tokens, gain, mask, fold)
 
 
 def project_kernel(
@@ -395,12 +408,6 @@
     ).reshape(slot_total, share, model_width)
     up_part = adapter_up_weight.reshape(slot_total, 2 * reduced_rows, local_width)
     active_slots = jnp.take(adapter_storage_slot, adapters_in_use, axis=0)
-    floats = tokens.astype(jnp.float32)
-    normed = (
-        floats
-        * lax.rsqrt(jnp.mean(floats * floats, axis=-1, keepdims=True) + norm_eps)
-        * input_norm_gain.astype(jnp.float32)
-    ).astype(jnp.bfloat16)
     relayed = req_total % 2 == 0 and req_total <= 16
     relayed = relayed and slot_total * req_total <= 2 * active_slots.shape[0]
     if relayed:
@@ -431,9 +438,15 @@
             output_weight,
         ]
         up_all, output_full, query_plain, key_base, value_plain, shrunk = relay_project(
-            arrays, normed, mask, fold, req_total, tp_total
+            arrays, tokens, input_norm_gain[None, :], mask, fold, req_total, tp_total
         )
     else:
+        floats = tokens.astype(jnp.float32)
+        normed = (
+            floats
+            * lax.rsqrt(jnp.mean(floats * floats, axis=-1, keepdims=True) + norm_eps)
+            * input_norm_gain.astype(jnp.float32)
+        ).astype(jnp.bfloat16)
         down_all = active_rows(down_part, active_slots)
         up_all = active_rows(up_part, active_slots)
         output_full = lax.all_gather(output_weight, "req", axis=1, tiled=True)

time: 163 us -> 170 us (1.043)
  local copies, waits for them, and re-layouts: 17.6 us -> 22.7 us
  matrix products: 14.9 us -> 17.4 us
    convert_element_type x2 -> x0, other arithmetic: 2.83 us -> none  [the longest x1 2.14 us: local(): normed = (floats * lax.rsqrt(jnp.mean(floats * floats, axis=-1, keepdims=...]
    pallas_call x1, local copies, waits for them, and re-layouts: 0.33 us -> 2.6 us  [relay_project(): pl.pallas_call(functools.partial(relay_kernel, lines, axes, (0, 1), tp_to...]
    another operation x3, other arithmetic: 0.68 us -> 2.86 us
    reduce_sum x1 -> x0, other arithmetic: 2.07 us -> none  [local(): jnp.mean(floats * floats, axis=-1, keepdims=True) + norm_eps]
    unnamed x37 -> x25, local copies, waits for them, and re-layouts: 10.6 us -> 10.8 us
where the time goes in v5:
time: 170 us; the launch traced here: 169 us
  Pallas kernels  121 us (71%)
  local copies, waits for them, and re-layouts  22.7 us (13%)
  matrix products  17.4 us (10%)
  other arithmetic  8.45 us (5%)
    pallas_call x1, Pallas kernels, relay_project(): pl.pallas_call(functools.partial(relay_kernel, lines, axes, (0, 1), tp_to...  104 us
    pallas_call x1, Pallas kernels, project_and_scatter(): pl.pallas_call(project_kernel, out_shape=jax.ShapeDtypeStruct(residual.sh...  16.2 us
    unnamed x25, local copies, waits for them, and re-layouts  10.8 us
    sub x1, matrix products, attend(): scores - row_peak  8.2 us
    dot_general x2, matrix products, change_of(): jnp.dot(spread, up_all[:, kind].reshape(place_total * reduced_rows, local...  5.02 us
    dot_general x1, matrix products, attend(): jnp.einsum('hqk,khd->qhd', weights, value_per_head, preferred_element_typ...  4.23 us

profile of v5, /device:TPU:0, one launch (start us, length us, event | category | flops | bytes accessed | tf_op | source)
XLA Modules:
  0.0 169.4 jit_solution(12809827368152254258)
XLA Ops:
  0.0 0.0 copy-start
  0.0 0.9 copy-done
  1.0 0.7 reshape_reshape.6.refs_0_
  1.6 0.7 broadcast_in_dim.43.refs_7_
  2.3 0.7 compare_select_fusion.1
  3.0 1.3 gather_fusion
  4.3 0.7 and_select_fusion.8
  5.0 0.7 fusion.47
  5.7 0.6 gather_fusion.1
  6.3 0.8 select_reduce_fusion
  7.1 0.1 compare_convert_fusion.refs_8_
  7.2 0.1 fusion.28.refs_9_
  7.3 0.0 copy-start.1
  7.3 1.6 copy-done.1
  8.9 0.9 copy-done.4
  9.9 0.9 copy-done.5
  10.8 0.9 copy-done.6
  11.8 0.9 copy-done.7
  12.7 0.8 copy-done.8
  13.5 0.8 copy-done.9
  14.4 104.4 %shard_map.118 = (bf16[8,64,512]{2,1,0:T(8,128)(2,1)S(1)}, bf16[512,2048]{1,0:T(8,128)(2,1)S(1)}, f32[512,512]{1,0:T(8,128)S(1)}, f32[512,512]{1,0:T(8,128)S(1)}...) custom-call(bf16[16,2048]{1,0:T(8,128)(2,1)S(1)} %copy-done.8, bf16[64,512]{1,0:T(8,128)(2,1)S(1)} %bitcast.27, ...), custom_call_target="tpu_custom_call" | custom-call | tf_op jit(solution)/shard_map/pallas_call | solution.py:213
  118.8 1.0 copy-done.2
  119.8 1.0 copy-done.3
  120.9 0.8 fusion.56
  121.7 0.5 fusion.45
  122.2 0.6 broadcast_compare_fusion
  122.8 2.2 %fusion.9 = bf16[512,512]{1,0:T(8,128)(2,1)} fusion(f32[512,512]{1,0:T(8,128)S(1)} %get-tuple-element.11, bf16[256,512]{1,0:T(8,128)(2,1)} %bitcast.31, s32[256]{0:T(256)S(1)} %get-tuple-element.34, s32[512]{0:T(512)S(1)} %select_reduce_fusion, bf16[512,128]{1,0:T(8,128)(2,1)S(1)} %get-tuple-element.12, s32[256]{0:T(256)S(1)} %get-tuple-element.33, ...), kind=kOutput, calls=%fused_computation.16 | convolution fusion | flops 143802368 | bytes 1970336 | tf_op jit(solution)/shard_map/dot_general | solution.py:483
  125.1 2.1 %copy.30 = bf16[512,512]{0,1:T(8,128)(2,1)} copy(bf16[512,512]{1,0:T(8,128)(2,1)} %fusion.9) | data formatting | bytes 1048576 | tf_op jit(solution)/shard_map/convert_element_type | solution.py:502
  127.2 0.0 copy-done.11
  127.2 0.9 fusion.12
  128.1 2.8 %fusion.6 = f32[512,512]{1,0:T(8,128)} fusion(f32[512,512]{1,0:T(8,128)} %copy-done.3, bf16[256,512]{1,0:T(8,128)(2,1)} %bitcast.30, s32[256]{0:T(256)S(1)} %get-tuple-element.34, s32[512]{0:T(512)S(1)} %select_reduce_fusion, bf16[512,128]{1,0:T(8,128)(2,1)S(1)} %get-tuple-element.12, s32[256]{0:T(256)S(1)} %get-tuple-element.33, s32[32]{0:T(128)} %fusion.45, ...), kind=kOutput, calls=%fused_computation.12 | convolution fusion | flops 143540224 | bytes 2494624 | tf_op jit(solution)/shard_map/dot_general | solution.py:483
  130.8 1.6 copy.32
  132.4 0.1 compare_reduce_fusion
  132.5 0.1 add_select_fusion
  132.6 0.3 reduce-window.9
  132.9 0.1 slice.42
  133.0 0.1 slice_reduce_fusion
  133.1 0.1 fusion.41
  133.2 0.3 multiply_cosine_fusion
  133.5 2.6 %copy.33 = f32[512,512]{0,1:T(8,128)} copy(f32[512,512]{1,0:T(8,128)} %copy-done.2) | data formatting | bytes 2097152 | tf_op jit(solution)/shard_map/pallas_call | solution.py:213
  136.1 2.5 %subtract_convert_fusion.1 = (bf16[512,8,32]{0,2,1:T(8,128)(2,1)}, bf16[512,8,32]{0,2,1:T(8,128)(2,1)}, bf16[512,8,32]{0,2,1:T(8,128)(2,1)}, bf16[512,8,32]{0,2,1:T(8,128)(2,1)}) fusion(f32[512,8,64]{0,2,1:T(8,128)S(1)} %bitcast.28, f32[512,32]{0,1:T(8,128)S(1)} %get-tuple-element.26, f32[512,32]{0,1:T(8,128)S(1)} %get-tuple-element.25, ...), kind=kLoop, calls=%fused_computation.31 | loop fusion | flops 2097152 | bytes 3276800 | tf_op jit(solution)/shard_map/convert.2
  138.6 8.2 %fusion.57 = (f32[8,512]{1,0:T(8,128)S(1)}, f32[8,512,512]{1,2,0:T(8,128)}) fusion(pred[512,512]{0,1:T(8,128)(4,1)} %fusion.12, bf16[512,8,32]{0,2,1:T(8,128)(2,1)} %get-tuple-element.23, bf16[512,8,32]{0,2,1:T(8,128)(2,1)} %get-tuple-element.24, bf16[512,8,32]{0,2,1:T(8,128)(2,1)} %get-tuple-element.18, bf16[512,8,32]{0,2,1:T(8,128)(2,1)} %get-tuple-element.17), kind=kOutput, calls=%fused_computation.106 | convolution fusion | flops 281018880 | bytes 9715712 | tf_op jit(solution)/shard_map/sub | solution.py:375
  146.8 0.0 copy-done.10
  146.8 4.2 %fusion.8 = bf16[8,64,512]{2,1,0:T(8,128)(2,1)S(1)} fusion(bf16[512,8,64]{0,2,1:T(8,128)(2,1)S(1)} %bitcast.32, f32[8,512,512]{1,2,0:T(8,128)} %get-tuple-element.28, f32[8,512]{1,0:T(8,128)S(1)} %get-tuple-element.27), kind=kOutput, calls=%fused_computation.15 | convolution fusion | flops 272891904 | bytes 9453568 | tf_op jit(solution)/shard_map/hqk,khd->qhd/dot_general | solution.py:377
  151.1 0.2 copy.35.attended
  151.3 1.1 constant_dynamic-slice_fusion.residual
  152.4 16.2 %shard_map.119 = bf16[512,512]{1,0:T(8,128)(2,1)S(1)} custom-call(bf16[512,512]{1,0:T(8,128)(2,1)S(1)} %copy.35.attended, bf16[512,2048]{1,0:T(8,128)(2,1)S(1)} %get-tuple-element.16.weight, bf16[512,512]{1,0:T(8,128)(2,1)S(1)} %constant_dynamic-slice_fusion.residual), custom_call_target="tpu_custom_call" | custom-call | tf_op jit(solution)/shard_map/pallas_call | solution.py:318
  168.6 0.8 copy.40
  (17 shorter events, 0.1 us)
Async XLA Ops:
  0.0 1.0 copy-start
  0.0 127.1 %copy-start.11 = (s32[1,512]{1,0:T(1,128)S(1)}, s32[1,512]{1,0:T(1,128)}, u32[]{:S(2)}) copy-start(s32[1,512]{1,0:T(1,128)} %param.13) | copy-start | bytes 6148
  7.3 1.6 copy-start.1
  8.9 0.9 copy-start.4
  9.9 0.9 copy-start.5
  10.8 0.9 copy-start.6
  11.8 0.9 copy-start.7
  12.7 0.8 copy-start.8
  13.5 0.8 copy-start.9
  118.8 1.0 copy-start.2
  119.8 1.0 copy-start.3
  138.6 8.2 %copy-start.10 = (bf16[512,512]{0,1:T(8,128)(2,1)S(1)}, bf16[512,512]{0,1:T(8,128)(2,1)}, u32[]{:S(2)}) copy-start(bf16[512,512]{0,1:T(8,128)(2,1)} %copy.30) | copy-start | bytes 1572868

commit v6 on v5

--- a/solution.py
+++ b/solution.py
@@ -236,7 +236,7 @@
             pltpu.SemaphoreType.DMA((tp_total - 1,)),
         ],
         compiler_params=pltpu.CompilerParams(
-            collective_id=0, has_side_effects=True, vmem_limit_bytes=40 * 1024 * 1024
+            collective_id=0, has_side_effects=True, vmem_limit_bytes=58 * 1024 * 1024
         ),
     )(*arrays, tokens, gain, mask, fold)
 

time: 170 us -> 156 us (0.918)
  local copies, waits for them, and re-layouts: 22.7 us -> 10 us
  Pallas kernels: 121 us -> 124 us
  matrix products: 17.4 us -> 14.7 us
  other arithmetic: 8.45 us -> 6.45 us
    unnamed x25 -> x11, local copies, waits for them, and re-layouts: 10.8 us -> 1.76 us
    pallas_call x1, Pallas kernels: 104 us -> 108 us  [relay_project(): pl.pallas_call(functools.partial(relay_kernel, lines, axes, (0, 1), tp_to...]
    pallas_call x1, local copies, waits for them, and re-layouts: 2.6 us -> 0.33 us  [relay_project(): pl.pallas_call(functools.partial(relay_kernel, lines, axes, (0, 1), tp_to...]
    another operation x3, other arithmetic: 2.86 us -> 0.69 us
where the time goes in v6:
time: 156 us
  Pallas kernels  124 us (79%)
  matrix products  14.7 us (9%)
  local copies, waits for them, and re-layouts  10 us (6%)
  other arithmetic  6.45 us (4%)
    pallas_call x1, Pallas kernels, relay_project(): pl.pallas_call(functools.partial(relay_kernel, lines, axes, (0, 1), tp_to...  108 us
    pallas_call x1, Pallas kernels, project_and_scatter(): pl.pallas_call(project_kernel, out_shape=jax.ShapeDtypeStruct(residual.sh...  16.2 us
    sub x1, matrix products, attend(): scores - row_peak  6.78 us
    dot_general x1, matrix products, attend(): jnp.einsum('hqk,khd->qhd', weights, value_per_head, preferred_element_typ...  4.38 us
    dot_general x2, matrix products, change_of(): jnp.dot(spread, up_all[:, kind].reshape(place_total * reduced_rows, local...  3.57 us

profile of v6, /device:TPU:0, one launch (start us, length us, event | category | flops | bytes accessed | tf_op | source)
XLA Modules:
  0.0 155.8 jit_solution(4858094719755457554)
XLA Ops:
  0.0 0.0 copy-start
  0.0 0.0 copy-start.4
  0.0 0.9 copy-done
  1.0 0.7 reshape_reshape.6.refs_0_
  1.6 1.3 broadcast_in_dim.43.refs_7_
  2.9 0.7 compare_select_fusion.1
  3.6 1.3 gather_fusion
  4.9 0.7 and_select_fusion.8
  5.6 0.7 fusion.47
  6.3 0.6 gather_fusion.1
  6.9 0.8 select_reduce_fusion
  7.7 0.8 compare_convert_fusion.refs_8_
  8.5 0.7 fusion.28.refs_9_
  9.1 108.2 %shard_map.118 = (bf16[8,64,512]{2,1,0:T(8,128)(2,1)}, bf16[512,2048]{1,0:T(8,128)(2,1)}, f32[512,512]{1,0:T(8,128)}, f32[512,512]{1,0:T(8,128)}, f32[512,512]{1,0:T(8,128)}, /*index=5*/bf16[512,128]{1,0:T(8,128)(2,1)}) custom-call(bf16[16,2048]{1,0:T(8,128)(2,1)} %reshape_reshape.6.refs_0_, bf16[64,512]{1,0:T(8,128)(2,1)} %bitcast.33, ...), custom_call_target="tpu_custom_call" | custom-call | tf_op jit(solution)/shard_map/pallas_call | solution.py:213
  117.4 0.0 copy-start.2
  117.4 1.2 fusion.56
  118.6 1.8 %fusion.9 = bf16[512,512]{1,0:T(8,128)(2,1)S(1)} fusion(f32[512,512]{1,0:T(8,128)} %get-tuple-element.11, bf16[256,512]{1,0:T(8,128)(2,1)S(1)} %bitcast.29, s32[256]{0:T(256)S(1)} %get-tuple-element.34, s32[512]{0:T(512)S(1)} %select_reduce_fusion, bf16[512,128]{1,0:T(8,128)(2,1)} %get-tuple-element.12, s32[256]{0:T(256)S(1)} %get-tuple-element.33, ...), kind=kOutput, calls=%fused_computation.16 | convolution fusion | flops 143802368 | bytes 1970336 | tf_op jit(solution)/shard_map/dot_general | solution.py:483
  120.4 1.0 copy.30
  121.4 0.0 copy-done.4
  121.4 0.9 fusion.12
  122.3 1.8 %fusion.6 = f32[512,512]{1,0:T(8,128)S(1)} fusion(f32[512,512]{1,0:T(8,128)} %get-tuple-element.14, bf16[256,512]{1,0:T(8,128)(2,1)S(1)} %bitcast.28, s32[256]{0:T(256)S(1)} %get-tuple-element.34, s32[512]{0:T(512)S(1)} %select_reduce_fusion, bf16[512,128]{1,0:T(8,128)(2,1)} %get-tuple-element.12, s32[256]{0:T(256)S(1)} %get-tuple-element.33, ...), kind=kOutput, calls=%fused_computation.12 | convolution fusion | flops 143540224 | bytes 2494624 | tf_op jit(solution)/shard_map/dot_general | solution.py:483
  124.1 0.3 copy.32
  124.4 0.1 compare_reduce_fusion
  124.5 0.1 add_select_fusion
  124.6 0.3 reduce-window.9
  124.9 0.1 slice.42
  125.0 0.1 slice_reduce_fusion
  125.2 0.1 fusion.41
  125.2 0.3 multiply_cosine_fusion
  125.5 0.0 copy-done.2
  125.6 0.3 copy.33
  125.9 0.3 subtract_convert_fusion.1
  126.2 0.0 copy-start.3
  126.3 6.8 %fusion.57 = (f32[8,512]{1,0:T(8,128)S(1)}, f32[8,512,512]{1,2,0:T(8,128)}) fusion(pred[512,512]{0,1:T(8,128)(4,1)} %fusion.12, bf16[512,8,32]{0,2,1:T(8,128)(2,1)S(1)} %get-tuple-element.23, bf16[512,8,32]{0,2,1:T(8,128)(2,1)S(1)} %get-tuple-element.24, bf16[512,8,32]{0,2,1:T(8,128)(2,1)S(1)} %get-tuple-element.18, ...), kind=kOutput, calls=%fused_computation.106 | convolution fusion | flops 281018880 | bytes 9715712 | tf_op jit(solution)/shard_map/sub | solution.py:375
  133.0 0.0 copy-done.3
  133.0 0.0 copy-start.1
  133.1 4.4 %fusion.8 = bf16[8,64,512]{2,1,0:T(8,128)(2,1)S(1)} fusion(bf16[512,8,64]{0,2,1:T(8,128)(2,1)S(1)} %bitcast.30, f32[8,512,512]{1,2,0:T(8,128)} %get-tuple-element.28, f32[8,512]{1,0:T(8,128)S(1)} %get-tuple-element.27), kind=kOutput, calls=%fused_computation.15 | convolution fusion | flops 272891904 | bytes 9453568 | tf_op jit(solution)/shard_map/hqk,khd->qhd/dot_general | solution.py:377
  137.4 0.2 copy.35.attended
  137.7 1.1 constant_dynamic-slice_fusion.residual
  138.7 0.0 copy-done.1
  138.8 16.2 %shard_map.119 = bf16[512,512]{1,0:T(8,128)(2,1)S(1)} custom-call(bf16[512,512]{1,0:T(8,128)(2,1)S(1)} %copy.35.attended, bf16[512,2048]{1,0:T(8,128)(2,1)S(1)} %copy-done.1, bf16[512,512]{1,0:T(8,128)(2,1)S(1)} %constant_dynamic-slice_fusion.residual), custom_call_target="tpu_custom_call" | custom-call | tf_op jit(solution)/shard_map/pallas_call | solution.py:318
  155.0 0.8 copy.40
  (9 shorter events, 0.1 us)
Async XLA Ops:
  0.0 1.0 copy-start
  0.0 121.4 %copy-start.4 = (s32[1,512]{1,0:T(1,128)S(1)}, s32[1,512]{1,0:T(1,128)}, u32[]{:S(2)}) copy-start(s32[1,512]{1,0:T(1,128)} %param.13) | copy-start | bytes 6148
  117.4 8.2 %copy-start.2 = (f32[512,512]{1,0:T(8,128)S(1)}, f32[512,512]{1,0:T(8,128)}, u32[]{:S(2)}) copy-start(f32[512,512]{1,0:T(8,128)} %get-tuple-element.15) | copy-start | bytes 3145732
  126.2 6.8 %copy-start.3 = (bf16[512,512]{0,1:T(8,128)(2,1)S(1)}, bf16[512,512]{0,1:T(8,128)(2,1)}, u32[]{:S(2)}) copy-start(bf16[512,512]{0,1:T(8,128)(2,1)} %copy.30) | copy-start | bytes 1572868
  133.0 5.7 %copy-start.1 = (bf16[512,2048]{1,0:T(8,128)(2,1)S(1)}, bf16[512,2048]{1,0:T(8,128)(2,1)}, u32[]{:S(2)}) copy-start(bf16[512,2048]{1,0:T(8,128)(2,1)} %get-tuple-element.16.weight) | copy-start | bytes 6291460
